TPU v7x, 128 devices: a whole 4x4x4 slice. The times are simulated.
128 devices in a mesh: row: 16 (over y, x_lo, core), col: 8 (over z, x_hi).
Axes of the slice: x: 4 (x_hi: 2, x_lo: 2; x = x_hi * 2 + x_lo), y: 4, z: 4, core: 2. Of those that a mesh axis runs over, the one named last changes fastest.
Arguments:
- homolog_activations: bfloat16 [256, 704, 256], P('row', 'col'), may hold values from -8 to 8
- coupling_activations: bfloat16 [704, 704, 128], P('row', 'col'), may hold values from -6 to 6
- homolog_existence_marks: int32 [256, 704], P('row', 'col'), may hold values from 0 to 1, as said below
- observed_peptide_marks: int32 [704], replicated, may hold values 0 or 1
- peptide_ordinals: int32 [704], replicated, may hold values from 1 to 2112, as said below
- strand_membership: int32 [704], replicated, may hold values from 0 to 7, never falling along the last dimension, each value on 1 to 176 neighbouring positions
- distance_ordinal_vectors: bfloat16 [66, 128], replicated, may hold values from -6 to 6
- coupling_score_mapping: bfloat16 [128, 8], replicated, may hold values from -0.5 to 0.5
- question_mapping_weights: bfloat16 [256, 256], replicated, may hold values from -4 to 4
- address_payload_mapping: bfloat16 [256, 512], replicated, may hold values from -4 to 4
- logistic_valve_mapping: bfloat16 [256, 256], replicated, may hold values from -0.375 to 0.375
- mixture_exit_mapping: bfloat16 [256, 256], replicated, may hold values from -0.375 to 0.375
- twofold_covariance_mapping: bfloat16 [256, 64], replicated, may hold values from -0.375 to 0.375
- covariance_exit_mapping: bfloat16 [1024, 128], replicated, may hold values from -0.1875 to 0.1875
- triad_opening_mappings: bfloat16 [128, 512], replicated, may hold values from -0.5 to 0.5
- triad_valve_mapping: bfloat16 [128, 128], replicated, may hold values from -0.5 to 0.5
- triad_exit_mapping: bfloat16 [128, 128], replicated, may hold values from -0.5 to 0.5
Outputs:
- homologs_after: bfloat16 [256, 704, 256], P('row', 'col')
- couplings_after: bfloat16 [704, 704, 128], P('row', 'col')
Inputs may be any that keep to these rules, and one draw needn't show every extreme that they name: Row 0 and column 0 of homolog_existence_marks are all ones. `peptide_ordinals`: strictly increasing along the residues.
All inputs are finite; a program needn't handle non-finite values.
Results may differ from a plain program's by a relative error of at most 0.008.
Values may be sent and summed in bfloat16 or wider, within the bound.
A program may use at most 192 MiB of HBM per device.

v0:
```python
import math

import jax
import jax.numpy as jnp
from jax import lax
from jax.sharding import PartitionSpec as P

REL_MAX = 32


norm_eps = 1e-05
count_eps = 0.001
masked_score = -1000000000.0


def broadcast(block, axis, holder):
    block = jnp.where(lax.axis_index(axis) == holder, block, jnp.zeros_like(block))
    return lax.psum(block, axis)


def zscore_transform(inputs):
    inputs = inputs.astype(jnp.float32)
    centred = inputs - jnp.mean(inputs, axis=-1, keepdims=True)
    spread = jnp.mean(centred * centred, axis=-1, keepdims=True)
    return centred * lax.rsqrt(spread + norm_eps)


def regrouped_covariance(operand, weights):
    batch_shape = operand.shape[:-1]
    result = jnp.dot(
        operand.reshape(-1, operand.shape[-1]), weights, preferred_element_type=jnp.float32
    )
    return result.reshape(batch_shape + (weights.shape[-1],))


def position_bins(index_rows, index_cols, chain_rows, chain_cols):
    offset = jnp.clip(index_rows[:, None] - index_cols[None, :] + REL_MAX, 0, 2 * REL_MAX)
    return jnp.where(chain_rows[:, None] == chain_cols[None, :], offset, 2 * REL_MAX + 1)


def shards(
    homolog_activations,
    coupling_activations,
    homolog_existence_marks,
    observed_peptide_marks,
    peptide_ordinals,
    strand_membership,
    distance_ordinal_vectors,
    coupling_score_mapping,
    question_mapping_weights,
    address_payload_mapping,
    logistic_valve_mapping,
    mixture_exit_mapping,
    twofold_covariance_mapping,
    covariance_exit_mapping,
    triad_opening_mappings,
    triad_valve_mapping,
    triad_exit_mapping,
):
    row_total = lax.axis_size("row")
    col_total = lax.axis_size("col")
    group_ratio = row_total // col_total
    row_place = lax.axis_index("row")
    col_place = lax.axis_index("col")
    tile_rows = coupling_activations.shape[0]
    block_columns = coupling_activations.shape[1]
    number_of_homologs = homolog_activations.shape[0]
    number_of_subspaces = coupling_score_mapping.shape[1]
    similarity_breadth = question_mapping_weights.shape[1]
    subspace_breadth = similarity_breadth // number_of_subspaces
    opm_width = twofold_covariance_mapping.shape[1] // 2
    tri_width = triad_exit_mapping.shape[0]
    row_first = row_place * tile_rows
    col_first = col_place * block_columns
    existing_homolog_marks = homolog_existence_marks.astype(jnp.float32)
    zscored_homologs = zscore_transform(homolog_activations).astype(jnp.bfloat16)
    covariance_source = (
        regrouped_covariance(zscored_homologs, twofold_covariance_mapping)
        * existing_homolog_marks[:, :, None]
    ).astype(jnp.bfloat16)
    every_seq, every_mask = (
        lax.all_gather(covariance_source, "row", axis=0, tiled=True),
        lax.all_gather(homolog_existence_marks, "row", axis=0, tiled=True),
    )
    offset = row_place % group_ratio * tile_rows
    left_source = lax.dynamic_slice_in_dim(every_seq[:, :, :opm_width], offset, tile_rows, 1)
    mask_source = lax.dynamic_slice_in_dim(every_mask, offset, tile_rows, 1)
    left_rows, mask_rows = (
        broadcast(left_source, "col", row_place // group_ratio),
        broadcast(mask_source, "col", row_place // group_ratio),
    )
    right_cols = every_seq[:, :, opm_width:]
    counts = jnp.dot(
        mask_rows.astype(jnp.bfloat16).T,
        every_mask.astype(jnp.bfloat16),
        preferred_element_type=jnp.float32,
    )
    outer_prod = jnp.einsum(
        "sic,sje->ijce", left_rows, right_cols, preferred_element_type=jnp.float32
    ).astype(jnp.bfloat16)
    mixed_opm = regrouped_covariance(
        outer_prod.reshape(tile_rows, block_columns, opm_width * opm_width), covariance_exit_mapping
    )
    outer_update = mixed_opm / (count_eps + counts[:, :, None])
    index_rows = lax.dynamic_slice_in_dim(peptide_ordinals, row_first, tile_rows)
    index_cols = lax.dynamic_slice_in_dim(peptide_ordinals, col_first, block_columns)
    chain_rows = lax.dynamic_slice_in_dim(strand_membership, row_first, tile_rows)
    chain_cols = lax.dynamic_slice_in_dim(strand_membership, col_first, block_columns)
    bucket = position_bins(index_rows, index_cols, chain_rows, chain_cols)
    one_hot = (
        bucket[:, :, None] == jnp.arange(distance_ordinal_vectors.shape[0], dtype=jnp.int32)
    ).astype(jnp.bfloat16)
    z_one = (
        coupling_activations.astype(jnp.float32)
        + regrouped_covariance(one_hot, distance_ordinal_vectors)
        + outer_update
    )
    ln_pair = zscore_transform(z_one)
    bias_tile = jnp.einsum(
        "ijc,ch->hij",
        ln_pair,
        coupling_score_mapping.astype(jnp.float32),
        precision=lax.Precision.HIGHEST,
    ).astype(jnp.bfloat16)
    ln_tri = ln_pair.astype(jnp.bfloat16)
    live_res_rows = lax.dynamic_slice_in_dim(observed_peptide_marks, row_first, tile_rows)
    live_res_cols = lax.dynamic_slice_in_dim(observed_peptide_marks, col_first, block_columns)
    pair_live = (live_res_rows[:, None] * live_res_cols[None, :]).astype(jnp.float32)[:, :, None]
    side_left = regrouped_covariance(ln_tri, triad_opening_mappings[:, : 2 * tri_width])
    tri_left = (
        jax.nn.sigmoid(side_left[:, :, tri_width:]) * side_left[:, :, :tri_width] * pair_live
    ).astype(jnp.bfloat16)
    side_right = regrouped_covariance(ln_tri, triad_opening_mappings[:, 2 * tri_width :])
    tri_right = (
        jax.nn.sigmoid(side_right[:, :, tri_width:]) * side_right[:, :, :tri_width] * pair_live
    ).astype(jnp.bfloat16)
    bias_wide, right_wide = (
        lax.all_gather(bias_tile, "col", axis=2, tiled=True),
        lax.all_gather(tri_right, "col", axis=1, tiled=True),
    )
    bias_parts = []
    right_parts = []
    for member in range(group_ratio):
        bias_piece, right_piece = (
            broadcast(bias_wide, "row", col_place * group_ratio + member),
            broadcast(right_wide, "row", col_place * group_ratio + member),
        )
        bias_parts.append(bias_piece)
        right_parts.append(right_piece)
    bias_query = jnp.concatenate(bias_parts, axis=1)
    right_rows = jnp.concatenate(right_parts, axis=0)
    queries = (
        regrouped_covariance(zscored_homologs, question_mapping_weights)
        .astype(jnp.bfloat16)
        .reshape(number_of_homologs, block_columns, number_of_subspaces, subspace_breadth)
    )
    gate_activation = jax.nn.sigmoid(regrouped_covariance(zscored_homologs, logistic_valve_mapping))
    score_scale = 1.0 / math.sqrt(subspace_breadth)
    key_value_pairs = regrouped_covariance(zscored_homologs, address_payload_mapping).astype(
        jnp.bfloat16
    )
    key_vals = lax.all_gather(key_value_pairs, "col", axis=1, tiled=True)
    existing_lookup_marks = lax.all_gather(homolog_existence_marks, "col", axis=1, tiled=True)
    left_piece = lax.all_gather(tri_left, "col", axis=1, tiled=True)
    maximal_precision = jnp.full(
        (number_of_homologs, number_of_subspaces, block_columns), -jnp.inf, jnp.float32
    )
    coefficient_accumulation = jnp.zeros(
        (number_of_homologs, number_of_subspaces, block_columns), jnp.float32
    )
    collected_slices = jnp.zeros(
        (number_of_homologs, number_of_subspaces, block_columns, subspace_breadth), jnp.float32
    )
    number_of_lookups = key_vals.shape[1]
    key_part = key_vals[:, :, :similarity_breadth].reshape(
        number_of_homologs, number_of_lookups, number_of_subspaces, subspace_breadth
    )
    value_part = key_vals[:, :, similarity_breadth:].reshape(
        number_of_homologs, number_of_lookups, number_of_subspaces, subspace_breadth
    )
    bias_block = bias_query.astype(jnp.float32)
    scores = (
        jnp.einsum("sihd,sjhd->shij", queries, key_part, preferred_element_type=jnp.float32)
        * score_scale
        + bias_block[None]
    )
    scores = jnp.where(existing_lookup_marks[:, None, None, :] > 0, scores, masked_score)
    newest = jnp.max(scores, axis=-1)
    shrink = jnp.exp(maximal_precision - newest)
    exp_terms = jnp.exp(scores - newest[..., None])
    coefficient_accumulation = coefficient_accumulation * shrink + jnp.sum(exp_terms, axis=-1)
    collected_slices = collected_slices * shrink[..., None] + jnp.einsum(
        "shij,sjhd->shid",
        exp_terms.astype(jnp.bfloat16),
        value_part,
        preferred_element_type=jnp.float32,
    )
    right_piece = right_rows
    crossed = jnp.einsum(
        "ikc,jkc->ijc", left_piece, right_piece, preferred_element_type=jnp.float32
    )
    outcome = (newest, coefficient_accumulation, collected_slices, crossed)
    maximal_precision, coefficient_accumulation, collected_slices, crossed = outcome
    softmax_mixture = collected_slices / coefficient_accumulation[..., None]
    softmax_mixture = softmax_mixture.transpose(0, 2, 1, 3).reshape(
        number_of_homologs, block_columns, similarity_breadth
    )
    filtered_attended_result = (gate_activation * softmax_mixture).astype(jnp.bfloat16)
    homologs_after = (
        homolog_activations.astype(jnp.float32)
        + regrouped_covariance(filtered_attended_result, mixture_exit_mapping)
    ).astype(jnp.bfloat16)
    normed_cross = zscore_transform(crossed).astype(jnp.bfloat16)
    tri_proj = regrouped_covariance(normed_cross, triad_exit_mapping)
    tri_gate = jax.nn.sigmoid(regrouped_covariance(ln_tri, triad_valve_mapping))
    couplings_after = (z_one + tri_gate * tri_proj).astype(jnp.bfloat16)
    return (homologs_after, couplings_after)


def solution(mesh):
    placed = (
        P("row", "col", None),
        P("row", "col", None),
        P("row", "col"),
        P(),
        P(),
        P(),
        P(),
        P(),
        P(),
        P(),
        P(),
        P(),
        P(),
        P(),
        P(),
        P(),
        P(),
    )
    return jax.shard_map(
        shards,
        mesh=mesh,
        in_specs=placed,
        out_specs=(P("row", "col", None), P("row", "col", None)),
        check_vma=False,
    )
```

profile of v0, /device:TPU:96, one launch (start us, length us, event | category | flops | bytes accessed | tf_op | source)
XLA Modules:
  0.0 1029.1 jit_solution(5595153346699519971)
XLA Ops:
  7.2 1.5 convert_reduce_fusion
  8.7 1.7 fusion.29
  11.1 2.5 fusion.34
  13.7 0.8 dynamic_slice.24
  15.2 0.8 dynamic_slice.25
  18.2 20.5 %all_gather.24 = s32[256,88]{1,0:T(8,128)S(1)} all-gather(s32[16,88]{1,0:T(8,128)S(1)} %copy-done.11), channel_id=1, replica_groups=mesh['row'=16,'col'=8] {'row'}, dimensions={0}, use_global_device_ids=true | all-gather | bytes 95744 | tf_op jit(solution)/shard_map/all_gather | solution.py:83
  38.8 14.0 %all-gather.8.cloned.1.call-done = bf16[256,88,64]{1,2,0:T(8,128)(2,1)} async-done(((bf16[16,88,64]{1,2,0:T(8,128)(2,1)}), bf16[256,88,64]{1,2,0:T(8,128)(2,1)}) %all-gather.8.cloned.1.call-update) | async-done | bytes 2883600 | tf_op jit(solution)/shard_map/all_gather | solution.py:82
  52.8 4.3 fusion.76
  57.8 1.8 copy.89
  59.5 0.9 broadcast_select_fusion.2
  60.5 42.3 %psum.43 = s32[256,44]{1,0:T(8,128)S(1)} all-reduce(s32[256,44]{1,0:T(8,128)S(1)} %dynamic-slice_select_fusion), channel_id=1, replica_groups=mesh['row'=16,'col'=8] {'col'}, use_global_device_ids=true, to_apply=%region_3.4 | all-reduce | flops 11264 | bytes 90112 | tf_op jit(solution)/shard_map/psum | solution.py:18
  103.2 3.7 copy.87
  106.9 41.7 %all-reduce.4.cloned.1.call-done = bf16[256,44,32]{0,1,2:T(8,128)(2,1)} async-done(((bf16[256,44,32]{0,1,2:T(8,128)(2,1)}), bf16[256,44,32]{0,1,2:T(8,128)(2,1)}) %all-reduce.4.cloned.1.call-update) | async-done | bytes 720912 | tf_op jit(solution)/shard_map/psum | solution.py:18
  148.6 11.3 %convolution_convert_fusion = bf16[88,32,44,32]{2,1,3,0:T(8,128)(2,1)} fusion(bf16[256,88,32]{0,2,1:T(8,128)(2,1)S(1)} %copy.87, bf16[256,44,32]{0,1,2:T(8,128)(2,1)} %all-reduce.4.cloned.1.call-done), kind=kOutput, calls=%fused_computation.8 | convolution fusion | flops 2034008064 | bytes 10092544 | tf_op jit(solution)/shard_map/sic,sje->ijce/dot_general | solution.py:98
  160.0 10.8 %fusion.51 = f32[44,88,128]{2,0,1:T(8,128)S(1)} fusion(bf16[44,88,1024]{0,2,1:T(8,128)(2,1)} %bitcast.88, bf16[1024,128]{1,0:T(8,128)(2,1)S(1)} %copy-done.9), kind=kOutput, calls=%fused_computation.72 | convolution fusion | flops 1015021568 | bytes 10174464 | tf_op jit(solution)/shard_map/dot_general | solution.py:30
  170.8 2.9 fusion.77
  173.8 1.4 multiply_reduce_fusion.1
  175.2 1.3 multiply_convert_fusion.1
  177.8 2.2 fusion.8
  180.6 2.8 convolution_convert_fusion.1
  183.5 2.7 fusion.38
  186.4 46.5 %all_gather.25 = bf16[8,44,704]{1,0,2:T(8,128)(2,1)S(1)} all-gather(bf16[8,44,88]{1,0,2:T(8,128)(2,1)S(1)} %copy.77), channel_id=1, replica_groups=mesh['row'=16,'col'=8] {'col'}, dimensions={2}, use_global_device_ids=true | all-gather | bytes 557568 | tf_op jit(solution)/shard_map/all_gather | solution.py:138
  232.9 1.9 copy.78
  234.9 2.2 broadcast_select_fusion.4
  237.0 57.8 %all-gather.10.cloned.1.call-done = bf16[44,704,128]{2,1,0:T(8,128)(2,1)} async-done(((bf16[44,88,128]{2,1,0:T(8,128)(2,1)}), bf16[44,704,128]{2,1,0:T(8,128)(2,1)}) %all-gather.10.cloned.1.call-update) | async-done | bytes 7929872 | tf_op jit(solution)/shard_map/all_gather | solution.py:139
  294.8 9.2 broadcast_select_fusion.1
  304.0 1.1 copy-done.5
  305.7 1.3 copy.71
  307.0 34.4 %all-gather = s32[8,88,16]{1,2,0:T(8,128)S(1)} all-gather(s32[1,88,16]{1,2,0:T(8,128)S(1)} %bitcast.96), channel_id=1, replica_groups=mesh['row'=16,'col'=8] {'col'}, dimensions={0}, use_global_device_ids=true | all-gather | bytes 50688 | tf_op jit(solution)/shard_map/all_gather | solution.py:163
  341.6 1.9 fusion.67
  343.5 55.5 %all-gather.12.cloned.1.call-done = bf16[44,704,128]{2,1,0:T(8,128)(2,1)} async-done(((bf16[44,88,128]{2,1,0:T(8,128)(2,1)}), bf16[44,704,128]{2,1,0:T(8,128)(2,1)}) %all-gather.12.cloned.1.call-update) | async-done | bytes 7929872 | tf_op jit(solution)/shard_map/all_gather | solution.py:164
  399.0 12.7 %copy.83 = bf16[44,704,128]{1,0,2:T(8,128)(2,1)} copy(bf16[44,704,128]{2,1,0:T(8,128)(2,1)} %all-gather.12.cloned.1.call-done) | data formatting | bytes 15859712 | tf_op jit(solution)/shard_map/all_gather | solution.py:164
  411.7 123.2 %all-gather.6.cloned.1.call-done = bf16[16,704,512]{2,1,0:T(8,128)(2,1)} async-done(((bf16[16,88,512]{2,1,0:T(8,128)(2,1)}), bf16[16,704,512]{2,1,0:T(8,128)(2,1)}) %all-gather.6.cloned.1.call-update) | async-done | bytes 11534352 | tf_op jit(solution)/shard_map/all_gather | solution.py:162
  534.9 9.8 fusion.75
  544.7 8.3 copy.72
  553.0 8.5 copy.80
  561.5 347.9 %all-reduce.6.cloned.1.call-done = (bf16[8,44,704]{2,1,0:T(8,128)(2,1)}, bf16[8,44,704]{2,1,0:T(8,128)(2,1)}, bf16[44,704,128]{2,1,0:T(8,128)(2,1)}, bf16[44,704,128]{2,1,0:T(8,128)(2,1)}) async-done(((bf16[8,44,704]{2,1,0:T(8,128)(2,1)}, bf16[8,44,704]{2,1,0:T(8,128)(2,1)}, bf16[44,704,128]{2,1,0:T(8,128)(2,1)}, bf16[44,704,128]{2,1,0:T(8,128)(2,1)}), (bf16[8,44,704]{2,1,0:T(8,128)(2,1)}, ...) | async-done | bytes 16850960 | tf_op jit(solution)/shard_map/psum | solution.py:18
  909.4 13.3 %pad_maximum_fusion = bf16[88,704,128]{2,1,0:T(8,128)(2,1)} fusion(bf16[44,704,128]{2,1,0:T(8,128)(2,1)} %get-tuple-element.4, bf16[44,704,128]{2,1,0:T(8,128)(2,1)} %get-tuple-element.5), kind=kLoop, calls=%fused_computation.7 | loop fusion | flops 7929856 | bytes 31719424 | tf_op jit(solution)/shard_map/concatenate | solution.py:151
  922.7 22.4 %copy.82 = bf16[88,704,128]{1,0,2:T(8,128)(2,1)} copy(bf16[88,704,128]{2,1,0:T(8,128)(2,1)} %pad_maximum_fusion) | data formatting | bytes 31719424 | tf_op jit(solution)/shard_map/concatenate | solution.py:151
  945.0 11.6 %bitcast_reduce_fusion = (f32[44,88]{1,0:T(8,128)S(1)}, f32[128,88,44]{1,2,0:T(8,128)S(1)}) fusion(bf16[88,704,128]{1,0,2:T(8,128)(2,1)} %copy.82, bf16[44,704,128]{1,0,2:T(8,128)(2,1)} %copy.83), kind=kOutput, calls=%fused_computation.12 | convolution fusion | flops 698319104 | bytes 25787520 | tf_op jit(solution)/shard_map/ikc,jkc->ijc/dot_general | solution.py:199
  957.1 1.5 multiply_convert_fusion
  958.9 1.0 copy-done.4
  959.9 17.1 %fusion.2 = (f32[16,8,88]{2,1,0:T(8,128)S(1)}, f32[16,8,88,704]{3,2,1,0:T(8,128)}) fusion(f32[8,88,704]{2,1,0:T(8,128)S(1)} %maximum_convert_fusion, pred[16,704]{1,0:T(8,128)(4,1)S(1)} %bitcast.93, bf16[16,88,8,32]{1,3,2,0:T(8,128)(2,1)S(1)} %bitcast.90, bf16[16,704,8,32]{1,3,2,0:T(8,128)(2,1)} %bitcast.89), kind=kOutput, calls=%fused_computation.4 | convolution fusion | flops 539218944 | bytes 40246272 | tf_op jit(solution)/shard_map/sihd,sjhd->shij/dot_general | solution.py:183
  977.0 16.4 %fusion = f32[16,8,88]{2,1,0:T(8,128)S(1)} fusion(f32[16,8,88,704]{3,2,1,0:T(8,128)} %get-tuple-element.19, f32[16,8,88]{2,1,0:T(8,128)S(1)} %get-tuple-element.18, f32[8,88,704]{2,1,0:T(8,128)S(1)} %maximum_convert_fusion, pred[16,704]{1,0:T(8,128)(4,1)S(1)} %bitcast.94), kind=kLoop, calls=%fused_computation.2 | loop fusion | flops 39638016 | bytes 33803264 | tf_op jit(solution)/shard_map/reduce_sum | solution.py:191
  993.4 18.9 %fusion.6 = f32[16,88,8,32]{1,3,2,0:T(8,128)} fusion(bf16[16,704,8,32]{1,3,2,0:T(8,128)(2,1)} %bitcast.91, f32[16,8,88,704]{3,2,1,0:T(8,128)} %get-tuple-element.19, f32[16,8,88]{2,1,0:T(8,128)S(1)} %get-tuple-element.18, f32[8,88,704]{2,1,0:T(8,128)S(1)} %maximum_convert_fusion, pred[16,704]{1,0:T(8,128)(4,1)S(1)} %bitcast.95, ...), kind=kOutput, calls=%fused_computation.19 | convolution fusion | flops 547880960 | bytes 41057280 | tf_op jit(solution)/shard_map/shij,sjhd->shid/dot_general | solution.py:192
  1012.3 2.9 copy.81
  1015.2 3.9 add_convert_fusion
  1019.1 3.1 fusion.33
  (77 shorter events, 8.7 us)
Async XLA Ops:
  7.2 173.5 %copy-start = (bf16[256,512]{1,0:T(8,128)(2,1)S(1)}, bf16[256,512]{1,0:T(8,128)(2,1)}, u32[]{:S(2)}) copy-start(bf16[256,512]{1,0:T(8,128)(2,1)} %param.26) | copy-start | bytes 786436
  7.2 11.0 %copy-start.11 = (s32[16,88]{1,0:T(8,128)S(1)}, s32[16,88]{1,0:T(8,128)}, u32[]{:S(2)}) copy-start(s32[16,88]{1,0:T(8,128)} %param.19) | copy-start | bytes 16900
  7.2 45.6 %all-gather.8.cloned.1.call-start = ((), (), s32[]{:S(2)}) async-start(), calls=%async_computation.1 | async-start | bytes 4456448 | tf_op jit(solution)/shard_map/all_gather | solution.py:82
  13.6 135.1 %all-reduce.4.cloned.1.call-start = ((), (), s32[]{:S(2)}) async-start(), calls=%async_computation.2 | async-start | bytes 1572864 | tf_op jit(solution)/shard_map/psum | solution.py:18
  60.5 234.3 %all-gather.10.cloned.1.call-start = ((), (), s32[]{:S(2)}) async-start(), calls=%async_computation.3 | async-start | bytes 8921088 | tf_op jit(solution)/shard_map/all_gather | solution.py:139
  106.9 53.1 %copy-start.9 = (bf16[1024,128]{1,0:T(8,128)(2,1)S(1)}, bf16[1024,128]{1,0:T(8,128)(2,1)}, u32[]{:S(2)}) copy-start(bf16[1024,128]{1,0:T(8,128)(2,1)} %param.30) | copy-start | bytes 786436
  160.0 10.8 %copy-start.14 = (bf16[44,88,128]{2,1,0:T(8,128)(2,1)S(1)}, bf16[44,88,128]{2,1,0:T(8,128)(2,1)}, u32[]{:S(2)}) copy-start(bf16[44,88,128]{2,1,0:T(8,128)(2,1)} %param.18) | copy-start | bytes 2973700
  160.0 10.8 %copy-start.19 = (bf16[66,128]{1,0:T(8,128)(2,1)S(1)}, bf16[66,128]{1,0:T(8,128)(2,1)}, u32[]{:S(2)}) copy-start(bf16[66,128]{1,0:T(8,128)(2,1)} %param.23) | copy-start | bytes 50692
  173.8 9.7 copy-start.2
  173.8 2.7 copy-start.10
  180.0 219.0 %all-gather.12.cloned.1.call-start = ((), (), s32[]{:S(2)}) async-start(), calls=%async_computation.4 | async-start | bytes 8921088 | tf_op jit(solution)/shard_map/all_gather | solution.py:164
  180.6 3.0 copy-start.13
  180.6 354.3 %all-gather.6.cloned.1.call-start = ((), (), s32[]{:S(2)}) async-start(), calls=%async_computation | async-start | bytes 12976128 | tf_op jit(solution)/shard_map/all_gather | solution.py:162
  183.5 725.9 %all-reduce.6.cloned.1.call-start = ((), (), s32[]{:S(2)}) async-start(), calls=%async_computation.5 | async-start | bytes 34078720 | tf_op jit(solution)/shard_map/psum | solution.py:18
  304.0 1.1 copy-start.5
  304.0 1.1 copy-start.15
  305.1 36.5 %copy-start.12 = (bf16[128,128]{1,0:T(8,128)(2,1)S(1)}, bf16[128,128]{1,0:T(8,128)(2,1)}, u32[]{:S(2)}) copy-start(bf16[128,128]{1,0:T(8,128)(2,1)} %param.32) | copy-start | bytes 98308
  957.1 1.6 copy-start.7
  957.1 1.6 copy-start.8
  958.7 1.2 copy-start.4
  1012.3 2.9 copy-start.3
  1012.3 2.9 copy-start.18
  1015.2 3.9 copy-start.6
  1015.2 3.9 copy-start.16
  1015.2 3.9 copy-start.17
  1019.1 3.1 copy-start.1
Sparse Core Ops, SparseCore 0:
  13.7 39.0 all-gather.7
  60.6 87.9 all-reduce.3
  180.1 114.6 all-gather.9
  297.8 101.1 all-gather.11
  401.5 133.3 all-gather.5
  538.3 371.0 all-reduce.5
where the time goes:
time: 1030 us
  waiting for transfers between devices  641 us (62%)
  blocking collectives  144 us (14%)
  matrix products  91.5 us (9%)
  local copies, waits for them, and re-layouts  85.3 us (8%)
  other arithmetic  53.2 us (5%)
  between operations  14.5 us (1%)
    psum x2, waiting for transfers between devices, broadcast(): return lax.psum(block, axis)  390 us
    all_gather x1, waiting for transfers between devices, shards(): key_vals = lax.all_gather(key_value_pairs, 'col', axis=1, tiled=True)  123 us
    all_gather x1, waiting for transfers between devices, shards(): lax.all_gather(tri_right, 'col', axis=1, tiled=True)  57.8 us
    all_gather x1, waiting for transfers between devices, shards(): left_piece = lax.all_gather(tri_left, 'col', axis=1, tiled=True)  55.5 us
    all_gather x1, blocking collectives, shards(): lax.all_gather(bias_tile, 'col', axis=2, tiled=True)  46.5 us
    psum x1, blocking collectives, broadcast(): return lax.psum(block, axis)  42.3 us
    all_gather x1, blocking collectives, shards(): lax.all_gather(homolog_existence_marks, 'col', axis=1, tiled=True)  34.4 us
    dot_general x10, matrix products, regrouped_covariance(): jnp.dot(operand.reshape(-1, operand.shape[-1]), weights, preferred_elemen...  29.8 us
  transfers between devices with their start and end apart: 6, of which 6 were waited for; matrix products, arithmetic and copies ran while one was open for 7% of the time, Pallas kernels for 0%

commit v1 on v0

v1 whole, which is shorter than its diff:
```python
import functools
import math

import jax
import jax.numpy as jnp
from jax import lax
from jax.experimental import pallas as pl
from jax.experimental.pallas import tpu as pltpu
from jax.sharding import PartitionSpec as P

REL_MAX = 32
norm_eps = 1e-05
count_eps = 0.001
masked_score = -1000000000.0
LOG2E = 1.4426950408889634
MESH = pl.DeviceIdType.MESH
BF = jnp.bfloat16
F32 = jnp.float32

NR, NC = 16, 8
SQ, RB, CB = 16, 44, 88
RP = 48
WR = 2816 + 128
WL = 1408 + 128


def norm(v):
    v = v.astype(F32)
    v = v - jnp.mean(v, axis=-1, keepdims=True)
    return v * lax.rsqrt(jnp.mean(v * v, axis=-1, keepdims=True) + norm_eps)


def dot(a, b):
    return jnp.dot(a, b, preferred_element_type=F32)


def dot_nt(a, b):
    return lax.dot_general(a, b, (((1,), (1,)), ((), ())), preferred_element_type=F32)


def msa_kernel(
    x_ref, xt_ref, mr_ref, ml_ref, wc_ref, wp_ref, qk_ref, rall_ref, lall_ref,
    rmsg, lmsg, lsem, ssem, rsem,
):
    r = lax.axis_index("row")
    c = lax.axis_index("col")
    own = (r // 2) == c
    bar = pltpu.get_barrier_semaphore()
    for k in range(1, NR):
        pl.semaphore_signal(bar, inc=1, device_id=(r ^ k, c), device_id_type=MESH)
    @pl.when(jnp.logical_not(own))
    def _():
        for q in range(NR):
            pl.semaphore_signal(bar, inc=1, device_id=(jnp.int32(q), r // 2), device_id_type=MESH)

    rmsg[:, 2816:] = mr_ref[...]
    lmsg[0, :, 1408:] = ml_ref[0]
    lmsg[1, :, 1408:] = ml_ref[1]
    for g in range(22):
        y = dot(norm(xt_ref[64 * g : 64 * g + 64, :]).astype(BF), wc_ref[...])
        right = jnp.concatenate([y[16 * t : 16 * t + 16, 32:] for t in range(4)], axis=1)
        left = jnp.concatenate([y[16 * t : 16 * t + 16, :32] for t in range(4)], axis=1)
        rmsg[:, 128 * g : 128 * g + 128] = right.astype(BF)
        lmsg[g // 11, :, 128 * (g % 11) : 128 * (g % 11) + 128] = left.astype(BF)

    pl.semaphore_wait(bar, NR - 1 + 2 * (NC - 1))
    for k in range(1, NR):
        pltpu.make_async_remote_copy(
            rmsg, rall_ref.at[r], ssem.at[0], rsem.at[0], device_id=(r ^ k, c), device_id_type=MESH
        ).start()
    for h in range(2):
        for b in range(NC):
            here = jnp.logical_and(own, jnp.logical_and(r % 2 == h, c == b))
            @pl.when(here)
            def _():
                pltpu.make_async_copy(lmsg.at[h], lall_ref.at[r], rsem.at[1]).start()
            @pl.when(jnp.logical_not(here))
            def _():
                pltpu.make_async_remote_copy(
                    lmsg.at[h], lall_ref.at[r], ssem.at[1], rsem.at[1],
                    device_id=(2 * c + h, jnp.int32(b)), device_id_type=MESH,
                ).start()
    mine = pltpu.make_async_copy(rmsg, rall_ref.at[r], lsem)
    mine.start()

    for sg in range(4):
        ys = []
        for t in range(4):
            s = 4 * sg + t
            ys.append(dot(norm(x_ref[CB * s : CB * s + CB, :]).astype(BF), wp_ref[...]))
        for kind in range(4):
            for h in range(8):
                at = kind * 256 + h * 32
                piece = jnp.concatenate([y[:, at : at + 32] for y in ys], axis=1)
                qk_ref[h, sg, :, 128 * kind : 128 * kind + 128] = piece.astype(BF)

    mine.wait()
    pltpu.make_async_copy(rall_ref.at[pl.ds(0, NR - 1)], rall_ref.at[pl.ds(0, NR - 1)], rsem.at[0]).wait()
    pltpu.make_async_copy(lall_ref, lall_ref, rsem.at[1]).wait()
    pltpu.make_async_copy(rall_ref.at[pl.ds(0, NR - 1)], rall_ref.at[pl.ds(0, NR - 1)], ssem.at[0]).wait()
    @pl.when(own)
    def _():
        pltpu.make_async_copy(lall_ref.at[pl.ds(0, NR - 1)], lall_ref.at[pl.ds(0, NR - 1)], ssem.at[1]).wait()
    @pl.when(jnp.logical_not(own))
    def _():
        pltpu.make_async_copy(lall_ref, lall_ref, ssem.at[1]).wait()


def msa_stage(x, xt, mr, ml, wc, wp):
    vm = pl.BlockSpec(memory_space=pltpu.VMEM)
    return pl.pallas_call(
        msa_kernel,
        out_shape=(
            jax.ShapeDtypeStruct((8, 4, CB, 512), BF),
            jax.ShapeDtypeStruct((NR, SQ, WR), BF),
            jax.ShapeDtypeStruct((NR, SQ, WL), BF),
        ),
        in_specs=[vm] * 6,
        out_specs=(vm,) * 3,
        scratch_shapes=[
            pltpu.VMEM((SQ, WR), BF),
            pltpu.VMEM((2, SQ, WL), BF),
            pltpu.SemaphoreType.DMA,
            pltpu.SemaphoreType.DMA((2,)),
            pltpu.SemaphoreType.DMA((2,)),
        ],
        compiler_params=pltpu.CompilerParams(
            collective_id=0, has_side_effects=True, vmem_limit_bytes=40 << 20
        ),
    )(x, xt, mr, ml, wc, wp)


def attention_kernel(qk_ref, bias_ref, madd_ref, out_ref, kbuf, vbuf):
    cb = pl.program_id(1)
    lane = lax.broadcasted_iota(jnp.int32, (CB, 128), 1) // 32

    @pl.when(cb == 0)
    def _():
        for b in range(NC):
            kbuf[CB * b : CB * b + CB, :] = qk_ref[b, 0, :, 128:256].astype(F32)
            vbuf[CB * b : CB * b + CB, :] = qk_ref[b, 0, :, 256:384].astype(F32)

    qg = qk_ref[cb, 0].astype(F32)
    keys = kbuf[...].astype(BF)
    vals = jnp.concatenate([vbuf[...].astype(BF), jnp.ones((704, 128), BF)], axis=1)
    bias = bias_ref[...].astype(F32)
    acc = jnp.zeros((CB, 128), F32)
    for t in range(4):
        q = jnp.where(lane == t, qg[:, :128], 0.0).astype(BF)
        s = dot_nt(q, keys) + bias + madd_ref[0, t : t + 1, :]
        p = jnp.exp2(s - jnp.max(s, axis=-1, keepdims=True)).astype(BF)
        o = dot(p, vals)
        acc = jnp.where(lane == t, o[:, :128] / o[:, 128:], acc)
    gate = jax.nn.sigmoid(qg[:, 384:])
    out_ref[0, 0] = (gate * acc).astype(BF)


def attention(qk, bias, madd):
    return pl.pallas_call(
        attention_kernel,
        out_shape=jax.ShapeDtypeStruct((NC, 4, CB, 128), BF),
        grid=(4, NC),
        in_specs=[
            pl.BlockSpec((NC, 1, CB, 512), lambda g, b: (0, g, 0, 0)),
            pl.BlockSpec((CB, 704), lambda g, b: (b, 0)),
            pl.BlockSpec((1, 4, 704), lambda g, b: (g, 0, 0)),
        ],
        out_specs=pl.BlockSpec((1, 1, CB, 128), lambda g, b: (b, g, 0, 0)),
        scratch_shapes=[pltpu.VMEM((704, 128), F32)] * 2,
        compiler_params=pltpu.CompilerParams(vmem_limit_bytes=40 << 20),
    )(qk, bias, madd)


def mix_kernel(g_ref, x_ref, w_ref, out_ref):
    lane = lax.broadcasted_iota(jnp.int32, (CB, 1024), 1) % 128 // 32
    cat = jnp.concatenate([g_ref[h, 0].astype(F32) for h in range(8)], axis=1)
    for t in range(4):
        y = dot(jnp.where(lane == t, cat, 0.0).astype(BF), w_ref[...])
        out_ref[t] = (x_ref[t].astype(F32) + y).astype(BF)


def mix(g, x, w):
    return pl.pallas_call(
        mix_kernel,
        out_shape=jax.ShapeDtypeStruct((SQ, CB, 256), BF),
        grid=(4,),
        in_specs=[
            pl.BlockSpec((8, 1, CB, 128), lambda g: (0, g, 0, 0)),
            pl.BlockSpec((4, CB, 256), lambda g: (g, 0, 0)),
            pl.BlockSpec((1024, 256), lambda g: (0, 0)),
        ],
        out_specs=pl.BlockSpec((4, CB, 256), lambda g: (g, 0, 0)),
    )(g, x, w)


def tri_kernel(t_ref, out_ref):
    for pair in range(4):
        acc = None
        for b in range(0, NC, 2):
            lhs = jnp.concatenate(
                [t_ref[:, b + d, 0].reshape(NR * RP, 128) for d in range(2)], axis=1
            )
            rhs = jnp.concatenate(
                [t_ref[4 * pair : 4 * pair + 4, b + d, 1].reshape(4 * RP, 128) for d in range(2)], axis=1
            )
            y = dot_nt(lhs, rhs)
            acc = y if acc is None else acc + y
        for h in range(2):
            at = 96 * h
            row = jnp.concatenate(
                [acc[:, at : at + 44], acc[:, at + 48 : at + 92], jnp.zeros((NR * RP, 40), F32)], axis=1
            )
            out_ref[:, 2 * pair + h] = row.astype(BF).reshape(NR, RP, 128)


def tri(t):
    vm = pl.BlockSpec(memory_space=pltpu.VMEM)
    return pl.pallas_call(
        tri_kernel,
        out_shape=jax.ShapeDtypeStruct((NR, NC, RP, 128), BF),
        in_specs=[vm],
        out_specs=vm,
        compiler_params=pltpu.CompilerParams(vmem_limit_bytes=40 << 20),
    )(t)


def flat_dot(operand, weights):
    result = dot(operand.reshape(-1, operand.shape[-1]), weights)
    return result.reshape(operand.shape[:-1] + (weights.shape[-1],))


def shards(
    msa, pair, marks, res_marks, ordinals, strand, dist_vectors, w_bias, w_q, w_kv, w_gate, w_mix,
    w_cov, w_opm, w_tri, w_valve, w_exit,
):
    r = lax.axis_index("row")
    c = lax.axis_index("col")
    marks_b = marks.astype(BF)
    xt = jnp.swapaxes(jnp.where(marks[:, :, None] > 0, msa, jnp.zeros_like(msa)), 0, 1)
    mr = jnp.pad(marks_b, ((0, 0), (0, 128 - CB)))
    ml = jnp.stack([jnp.pad(marks_b[:, RB * h : RB * h + RB], ((0, 0), (0, 128 - RB))) for h in range(2)])
    scale = LOG2E / math.sqrt(32.0)
    wp = jnp.concatenate([(w_q.astype(F32) * scale).astype(BF), w_kv, w_gate], axis=1)
    qk, rall, lall = msa_stage(
        msa.reshape(SQ * CB, 256), xt.reshape(SQ * CB, 256), mr, ml, w_cov, wp
    )
    qk = lax.all_to_all(qk, "col", 0, 0, tiled=True)
    every_marks = lax.all_gather(marks, "col", axis=1, tiled=True)
    madd = jnp.where(every_marks > 0, 0.0, masked_score).astype(F32).reshape(4, 4, 704)

    rall = rall.reshape(256, WR)
    lall = lall.reshape(256, WL)
    counts = dot(lall[:, 1408 : 1408 + RB].T, rall[:, 2816 : 2816 + CB])
    outer = jnp.einsum(
        "sic,sje->ijce",
        lall[:, :1408].reshape(256, RB, 32),
        rall[:, :2816].reshape(256, CB, 32),
        preferred_element_type=F32,
    ).astype(BF)
    update = flat_dot(outer.reshape(RB, CB, 1024), w_opm) / (count_eps + counts[:, :, None])
    row_first, col_first = r * RB, c * CB
    cut_r = lambda v: lax.dynamic_slice_in_dim(v, row_first, RB)
    cut_c = lambda v: lax.dynamic_slice_in_dim(v, col_first, CB)
    bins = jnp.clip(cut_r(ordinals)[:, None] - cut_c(ordinals)[None, :] + REL_MAX, 0, 2 * REL_MAX)
    bins = jnp.where(cut_r(strand)[:, None] == cut_c(strand)[None, :], bins, 2 * REL_MAX + 1)
    one_hot = (bins[:, :, None] == jnp.arange(dist_vectors.shape[0], dtype=jnp.int32)).astype(BF)
    z_one = pair.astype(F32) + flat_dot(one_hot, dist_vectors) + update
    ln_pair = norm(z_one)
    bias = jnp.einsum("ijc,ch->hij", ln_pair, w_bias.astype(F32), precision=lax.Precision.HIGHEST)
    bias = (bias * LOG2E).astype(BF)
    bias = lax.all_to_all(bias, "col", 0, 0, tiled=True)
    bias = lax.all_gather(bias, "row", axis=0, tiled=False)
    bias = bias.transpose(0, 2, 1, 3).reshape(704, 704)

    ln_tri = ln_pair.astype(BF)
    live = (cut_r(res_marks)[:, None] * cut_c(res_marks)[None, :]).astype(F32)
    side = jnp.einsum("ijc,cd->dij", ln_tri, w_tri, preferred_element_type=F32)
    t_left = (jax.nn.sigmoid(side[128:256]) * side[:128] * live).astype(BF)
    t_right = (jax.nn.sigmoid(side[384:]) * side[256:384] * live).astype(BF)
    both = jnp.stack([t_left, t_right], axis=1)
    both = jnp.pad(both, ((0, 0), (0, 0), (0, RP - RB), (0, 128 - CB)))
    both = lax.all_to_all(both, ("row", "col"), 0, 0, tiled=True)
    crossed = tri(both.reshape(NR, NC, 2, RP, 128))
    crossed = lax.all_to_all(crossed.reshape(128, RP, 128), ("row", "col"), 0, 0, tiled=True)
    crossed = crossed[:, :RB, :CB].astype(F32)
    crossed = crossed - jnp.mean(crossed, axis=0, keepdims=True)
    crossed = crossed * lax.rsqrt(jnp.mean(crossed * crossed, axis=0, keepdims=True) + norm_eps)
    proj = jnp.einsum("cij,cf->ijf", crossed.astype(BF), w_exit, preferred_element_type=F32)
    gate = jax.nn.sigmoid(flat_dot(ln_tri, w_valve))
    pair_out = (z_one + gate * proj).astype(BF)

    gated = attention(qk, bias, madd)
    gated = lax.all_to_all(gated, "col", 0, 0, tiled=True)
    w_rep = jnp.broadcast_to(w_mix.reshape(8, 1, 32, 256), (8, 4, 32, 256)).reshape(1024, 256)
    return mix(gated, msa, w_rep), pair_out


def solution(mesh):
    placed = (P("row", "col", None), P("row", "col", None), P("row", "col")) + (P(),) * 14
    return jax.shard_map(
        shards,
        mesh=mesh,
        in_specs=placed,
        out_specs=(P("row", "col", None), P("row", "col", None)),
        check_vma=False,
    )
```

time: 1030 us -> 366 us (0.36)
  waiting for transfers between devices: 641 us -> 43.2 us
  Pallas kernels: 0 us -> 112 us
  matrix products: 91.5 us -> 33.9 us
  local copies, waits for them, and re-layouts: 85.3 us -> 30.3 us
  blocking collectives: 144 us -> 101 us
  other arithmetic: 53.2 us -> 13 us
  starting transfers between devices: 0.24 us -> 26.6 us
  between operations: 14.5 us -> 1.06 us
    psum x2 -> x0, waiting for transfers between devices: 390 us -> none  [broadcast(): return lax.psum(block, axis)]
    all_gather x4 -> x0, waiting for transfers between devices: 250 us -> none  [the longest x1 123 us: shards(): key_vals = lax.all_gather(key_value_pairs, 'col', axis=1, tiled=True)]
    pallas_call x0 -> x4, Pallas kernels: none -> 112 us  [the longest x1 56.1 us: msa_stage(): pl.pallas_call(msa_kernel, out_shape=(jax.ShapeDtypeStruct((8, 4, CB, 512...]
    dot_general x16 -> x8, matrix products: 91.5 us -> 33.9 us  [the longest x4 16.4 us: dot(): return jnp.dot(a, b, preferred_element_type=F32)]
    all_to_all x0 -> x4, waiting for transfers between devices: none -> 43.2 us  [the longest x1 19.7 us: shards(): qk = lax.all_to_all(qk, 'col', 0, 0, tiled=True)]
    psum x1 -> x0, blocking collectives: 42.3 us -> none  [broadcast(): return lax.psum(block, axis)]
    slice x4, local copies, waits for them, and re-layouts: 30.9 us -> 2.05 us  [the longest x1 1.18 us: shards(): lall[:, :1408].reshape(256, RB, 32)]
    all_to_all x0 -> x4, starting transfers between devices: none -> 26.6 us  [the longest x1 7.64 us: shards(): lax.all_to_all(crossed.reshape(128, RP, 128), ('row', 'col'), 0, 0, tiled...]
  transfers between devices with their start and end apart: 6 -> 4, of which waited for: 6 -> 3; matrix products, arithmetic and copies ran while one was open for 7% -> 7% of each run, Pallas kernels for 0% -> 15%
where the time goes in v1:
time: 366 us; the launch traced here: 361 us
  Pallas kernels  112 us (31%)
  blocking collectives  101 us (28%)
  waiting for transfers between devices  43.2 us (12%)
  matrix products  33.9 us (9%)
  local copies, waits for them, and re-layouts  30.3 us (8%)
  starting transfers between devices  26.6 us (7%)
  other arithmetic  13 us (4%)
    all_gather x1, blocking collectives, shards(): every_marks = lax.all_gather(marks, 'col', axis=1, tiled=True)  63.9 us
    pallas_call x1, Pallas kernels, msa_stage(): pl.pallas_call(msa_kernel, out_shape=(jax.ShapeDtypeStruct((8, 4, CB, 512...  56.1 us
    pallas_call x1, Pallas kernels, attention(): pl.pallas_call(attention_kernel, out_shape=jax.ShapeDtypeStruct((NC, 4, C...  49 us
    all_gather x1, blocking collectives, shards(): bias = lax.all_gather(bias, 'row', axis=0, tiled=False)  26.1 us
    all_to_all x1, waiting for transfers between devices, shards(): qk = lax.all_to_all(qk, 'col', 0, 0, tiled=True)  19.7 us
    dot_general x4, matrix products, dot(): return jnp.dot(a, b, preferred_element_type=F32)  16.4 us
    all_to_all x1, waiting for transfers between devices, shards(): lax.all_to_all(crossed.reshape(128, RP, 128), ('row', 'col'), 0, 0, tiled...  14.5 us
    unnamed x51, local copies, waits for them, and re-layouts  13.4 us
  transfers between devices with their start and end apart: 4, of which 3 were waited for; matrix products, arithmetic and copies ran while one was open for 7% of the time, Pallas kernels for 15%

profile of v1, /device:TPU:96, one launch (start us, length us, event | category | flops | bytes accessed | tf_op | source)
XLA Modules:
  0.0 361.1 jit_solution(7000788775871132111)
XLA Ops:
  0.7 0.8 broadcast_compare_fusion
  1.5 0.7 convert_element_type.58
  2.2 1.4 select_bitcast_fusion
  4.1 56.1 %shard_map.176 = (bf16[8,4,88,512]{3,2,1,0:T(8,128)(2,1)S(1)}, bf16[16,16,2944]{2,1,0:T(8,128)(2,1)S(1)}, bf16[16,16,1536]{2,1,0:T(8,128)(2,1)S(1)}) custom-call(bf16[1408,256]{1,0:T(8,128)(2,1)S(1)} %bitcast.70, bf16[1408,256]{1,0:T(8,128)(2,1)S(1)} %bitcast.72, bf16[16,128]{1,0:T(8,128)(2,1)S(1)} %pad.15.mr_ref, ...), custom_call_target="tpu_custom_call" | custom-call | tf_op jit(solution)/shard_map/pallas_call | solution.py:111
  60.5 1.2 slice.47
  62.1 0.8 dynamic_slice.21
  62.8 0.8 dynamic_slice.20
  63.6 0.8 dynamic_slice.19
  64.4 0.8 dynamic_slice.18
  65.8 1.4 copy.63
  67.2 10.1 %convolution_convert_fusion = bf16[88,32,44,32]{2,1,3,0:T(8,128)(2,1)} fusion(bf16[256,88,32,1]{0,2,3,1:T(8,128)(2,1)S(1)} %bitcast.78, bf16[256,44,32]{0,2,1:T(8,128)(2,1)S(1)} %bitcast.79), kind=kOutput, calls=%fused_computation | convolution fusion | flops 2034008064 | bytes 10092544 | tf_op jit(solution)/shard_map/sic,sje->ijce/dot_general | solution.py:254
  77.4 10.8 %fusion.36 = f32[44,88,128]{2,0,1:T(8,128)S(1)} fusion(bf16[44,88,1024]{0,2,1:T(8,128)(2,1)} %bitcast.77, bf16[1024,128]{1,0:T(8,128)(2,1)S(1)} %copy-done), kind=kOutput, calls=%fused_computation.48 | convolution fusion | flops 1015021568 | bytes 10174464 | tf_op jit(solution)/shard_map/dot_general | solution.py:34
  88.3 2.9 fusion.47
  91.3 1.4 multiply_reduce_fusion
  92.7 2.9 fusion.26
  95.6 11.2 %all_to_all.25 = bf16[8,44,88]{2,1,0:T(8,128)(2,1)S(1)} all-to-all(bf16[8,44,88]{2,1,0:T(8,128)(2,1)S(1)} %copy.55), channel_id=1, replica_groups=mesh['row'=16,'col'=8] {'col'}, dimensions={0} | all-to-all | bytes 123904 | tf_op jit(solution)/shard_map/all_to_all | solution.py:271
  106.8 6.0 %all-to-all-start = ((bf16[8,4,88,512]{3,2,1,0:T(8,128)(2,1)}), bf16[8,4,88,512]{3,2,1,0:T(8,128)(2,1)S(1)}, u32[]{:S(2)}, u32[]{:S(2)}) async-start(bf16[8,4,88,512]{3,2,1,0:T(8,128)(2,1)} %copy-done.8), calls=%async_computation | async-start | bytes 5767168 | tf_op jit(solution)/shard_map/all_to_all | solution.py:247
  112.8 0.8 dynamic_slice.23
  113.6 0.8 dynamic_slice.22
  114.4 2.7 convolution_bitcast_fusion
  117.2 1.3 fusion.31
  118.5 1.5 pad_maximum_fusion
  120.0 4.8 %copy.64 = bf16[128,2,44,88]{3,2,1,0:T(8,128)(2,1)} copy(bf16[128,2,44,88]{0,3,2,1:T(8,128)(2,1)} %pad_maximum_fusion) | data formatting | bytes 3964928
  124.7 4.2 %pad.18.clone = bf16[128,2,48,128]{3,2,1,0:T(8,128)(2,1)} pad(bf16[128,2,44,88]{3,2,1,0:T(8,128)(2,1)} %copy.64, bf16[]{:T(256)} %constant.20.clone.1), padding=0_0x0_0x0_4x0_40 | pad | bytes 5128194 | tf_op jit(solution)/shard_map/jit(_pad)/pad | solution.py:281
  128.9 19.7 %all-to-all-done.qk_ref = bf16[8,4,88,512]{3,2,1,0:T(8,128)(2,1)S(1)} async-done(((bf16[8,4,88,512]{3,2,1,0:T(8,128)(2,1)}), bf16[8,4,88,512]{3,2,1,0:T(8,128)(2,1)S(1)}, u32[]{:S(2)}, u32[]{:S(2)}) %all-to-all-start) | async-done | bytes 2883616 | tf_op jit(solution)/shard_map/all_to_all | solution.py:247
  148.6 1.6 copy-done.2
  150.2 6.1 %all-to-all-start.3 = ((bf16[128,2,48,128]{3,2,1,0:T(8,128)(2,1)}), bf16[128,2,48,128]{3,2,1,0:T(8,128)(2,1)S(1)}, u32[]{:S(2)}, u32[]{:S(2)}) async-start(bf16[128,2,48,128]{3,2,1,0:T(8,128)(2,1)} %pad.18.clone), calls=%async_computation.3 | async-start | bytes 6291456 | tf_op jit(solution)/shard_map/all_to_all | solution.py:282
  156.3 63.9 %all-gather.1 = s32[8,88,16]{1,2,0:T(8,128)S(1)} all-gather(s32[1,88,16]{1,2,0:T(8,128)S(1)} %bitcast.83), channel_id=1, replica_groups=mesh['row'=16,'col'=8] {'col'}, dimensions={0}, use_global_device_ids=true | all-gather | bytes 50688 | tf_op jit(solution)/shard_map/all_gather | solution.py:248
  220.4 26.1 %all-gather = bf16[128,44,88]{2,0,1:T(8,128)(2,1)S(1)} all-gather(bf16[8,44,88]{2,0,1:T(8,128)(2,1)S(1)} %copy.56), channel_id=2, replica_groups=mesh['row'=16,'col'=8] {'row'}, dimensions={0}, use_global_device_ids=true | all-gather | bytes 1053184 | tf_op jit(solution)/shard_map/all_gather | solution.py:272
  246.5 1.4 copy_bitcast_fusion
  247.9 3.6 reshape.178.bias_ref
  251.5 1.8 copy-done.3
  253.3 1.2 copy-done.6
  254.6 49.0 %shard_map.177 = bf16[8,4,88,128]{3,2,1,0:T(8,128)(2,1)S(1)} custom-call(bf16[8,4,88,512]{3,2,1,0:T(8,128)(2,1)S(1)} %copy-done.3, bf16[704,704]{1,0:T(8,128)(2,1)S(1)} %copy-done.6, f32[4,4,704]{2,1,0:T(4,128)S(1)} %reshape.179.madd_ref), custom_call_target="tpu_custom_call" | custom-call | tf_op jit(solution)/shard_map/pallas_call | solution.py:159
  303.6 0.8 copy-done.7
  304.5 6.8 %all-to-all-start.2 = ((bf16[8,4,88,128]{3,2,1,0:T(8,128)(2,1)}), bf16[8,4,88,128]{3,2,1,0:T(8,128)(2,1)}, u32[]{:S(2)}, u32[]{:S(2)}) async-start(bf16[8,4,88,128]{3,2,1,0:T(8,128)(2,1)} %copy-done.7), calls=%async_computation.2 | async-start | bytes 1441792 | tf_op jit(solution)/shard_map/all_to_all | solution.py:293
  311.3 2.1 shard_map.179
  313.4 1.2 copy-done.5
  314.5 8.9 %all-to-all-done.2.g_ref = bf16[8,4,88,128]{3,2,1,0:T(8,128)(2,1)} async-done(((bf16[8,4,88,128]{3,2,1,0:T(8,128)(2,1)}), bf16[8,4,88,128]{3,2,1,0:T(8,128)(2,1)}, u32[]{:S(2)}, u32[]{:S(2)}) %all-to-all-start.2) | async-done | bytes 720928 | tf_op jit(solution)/shard_map/all_to_all | solution.py:293
  323.5 7.6 %all-to-all-start.4 = ((bf16[128,48,128]{2,1,0:T(8,128)(2,1)}), bf16[128,48,128]{2,1,0:T(8,128)(2,1)}, u32[]{:S(2)}, u32[]{:S(2)}) async-start(bf16[128,48,128]{2,1,0:T(8,128)(2,1)} %bitcast.71), calls=%async_computation.4 | async-start | bytes 3145728 | tf_op jit(solution)/shard_map/all_to_all | solution.py:284
  331.2 2.4 fusion.38
  333.6 0.9 broadcast_in_dim.52
  334.4 4.6 %shard_map.178 = bf16[16,88,256]{2,1,0:T(8,128)(2,1)} custom-call(bf16[8,4,88,128]{3,2,1,0:T(8,128)(2,1)} %all-to-all-done.2.g_ref, bf16[16,88,256]{2,1,0:T(8,128)(2,1)} %x_ref.1, bf16[1024,256]{1,0:T(8,128)(2,1)} %bitcast.80), custom_call_target="tpu_custom_call" | custom-call | tf_op jit(solution)/shard_map/pallas_call | solution.py:183
  339.0 14.5 %all-to-all-done.4 = bf16[128,48,128]{2,1,0:T(8,128)(2,1)} async-done(((bf16[128,48,128]{2,1,0:T(8,128)(2,1)}), bf16[128,48,128]{2,1,0:T(8,128)(2,1)}, u32[]{:S(2)}, u32[]{:S(2)}) %all-to-all-start.4) | async-done | bytes 1572896 | tf_op jit(solution)/shard_map/all_to_all | solution.py:284
  353.5 1.8 convert_reduce_fusion
  355.3 2.0 fusion.2
  357.3 2.0 fusion.3
  359.3 1.8 add_convert_fusion
  (67 shorter events, 2.2 us)
Async XLA Ops:
  0.6 76.7 %copy-start = (bf16[1024,128]{1,0:T(8,128)(2,1)S(1)}, bf16[1024,128]{1,0:T(8,128)(2,1)}, u32[]{:S(2)}) copy-start(bf16[1024,128]{1,0:T(8,128)(2,1)} %param.30) | copy-start | bytes 786436
  0.6 3.2 copy-start.19
  0.7 3.3 copy-start.15
  0.7 3.4 copy-start.16
  0.7 3.4 copy-start.12
  2.2 1.9 copy-start.4
  60.3 1.8 copy-start.8
  77.3 10.9 %copy-start.21 = (bf16[44,88,128]{2,1,0:T(8,128)(2,1)S(1)}, bf16[44,88,128]{2,1,0:T(8,128)(2,1)}, u32[]{:S(2)}) copy-start(bf16[44,88,128]{2,1,0:T(8,128)(2,1)} %param.18) | copy-start | bytes 2973700
  77.4 10.9 %copy-start.23 = (bf16[66,128]{1,0:T(8,128)(2,1)S(1)}, bf16[66,128]{1,0:T(8,128)(2,1)}, u32[]{:S(2)}) copy-start(bf16[66,128]{1,0:T(8,128)(2,1)} %param.23) | copy-start | bytes 50692
  91.2 4.3 %copy-start.9 = (f32[44,88,128]{2,1,0:T(8,128)}, f32[44,88,128]{2,1,0:T(8,128)S(1)}, u32[]{:S(2)}) copy-start(f32[44,88,128]{2,1,0:T(8,128)S(1)} %get-tuple-element.13) | copy-start | bytes 5947396
  91.2 1.4 copy-start.20
  106.8 7.6 %copy-start.13 = (bf16[128,512]{1,0:T(8,128)(2,1)S(1)}, bf16[128,512]{1,0:T(8,128)(2,1)}, u32[]{:S(2)}) copy-start(bf16[128,512]{1,0:T(8,128)(2,1)} %param.31) | copy-start | bytes 393220
  106.8 41.8 %all-to-all-start = ((bf16[8,4,88,512]{3,2,1,0:T(8,128)(2,1)}), bf16[8,4,88,512]{3,2,1,0:T(8,128)(2,1)S(1)}, u32[]{:S(2)}, u32[]{:S(2)}) async-start(bf16[8,4,88,512]{3,2,1,0:T(8,128)(2,1)} %copy-done.8), calls=%async_computation | async-start | bytes 5767168 | tf_op jit(solution)/shard_map/all_to_all | solution.py:247
  128.9 27.4 %copy-start.17 = (s32[16,88]{1,0:T(8,128)S(1)}, s32[16,88]{1,0:T(8,128)}, u32[]{:S(2)}) copy-start(s32[16,88]{1,0:T(8,128)} %param.19) | copy-start | bytes 16900
  148.6 1.6 copy-start.2
  150.2 154.3 %all-to-all-start.3 = ((bf16[128,2,48,128]{3,2,1,0:T(8,128)(2,1)}), bf16[128,2,48,128]{3,2,1,0:T(8,128)(2,1)S(1)}, u32[]{:S(2)}, u32[]{:S(2)}) async-start(bf16[128,2,48,128]{3,2,1,0:T(8,128)(2,1)} %pad.18.clone), calls=%async_computation.3 | async-start | bytes 6291456 | tf_op jit(solution)/shard_map/all_to_all | solution.py:282
  251.5 1.8 copy-start.3
  253.3 1.2 copy-start.6
  303.6 0.9 copy-start.7
  304.5 19.0 %all-to-all-start.2 = ((bf16[8,4,88,128]{3,2,1,0:T(8,128)(2,1)}), bf16[8,4,88,128]{3,2,1,0:T(8,128)(2,1)}, u32[]{:S(2)}, u32[]{:S(2)}) async-start(bf16[8,4,88,128]{3,2,1,0:T(8,128)(2,1)} %copy-done.7), calls=%async_computation.2 | async-start | bytes 1441792 | tf_op jit(solution)/shard_map/all_to_all | solution.py:293
  313.4 1.2 copy-start.5
  314.5 16.6 %copy-start.10 = (f32[44,88,128]{2,1,0:T(8,128)S(1)}, f32[44,88,128]{2,1,0:T(8,128)}, u32[]{:S(2)}) copy-start(f32[44,88,128]{2,1,0:T(8,128)} %copy-done.9) | copy-start | bytes 5947396
  314.5 16.6 %copy-start.18 = (bf16[128,128]{1,0:T(8,128)(2,1)S(1)}, bf16[128,128]{1,0:T(8,128)(2,1)}, u32[]{:S(2)}) copy-start(bf16[128,128]{1,0:T(8,128)(2,1)} %param.32) | copy-start | bytes 98308
  323.5 30.1 %all-to-all-start.4 = ((bf16[128,48,128]{2,1,0:T(8,128)(2,1)}), bf16[128,48,128]{2,1,0:T(8,128)(2,1)}, u32[]{:S(2)}, u32[]{:S(2)}) async-start(bf16[128,48,128]{2,1,0:T(8,128)(2,1)} %bitcast.71), calls=%async_computation.4 | async-start | bytes 3145728 | tf_op jit(solution)/shard_map/all_to_all | solution.py:284
  331.1 2.4 copy-start.14
  357.3 2.0 copy-start.11
  357.3 2.0 copy-start.22
  359.3 1.8 copy-start.1

commit v2 on v1

v2 whole, which is shorter than its diff:
```python
import math

import jax
import jax.numpy as jnp
from jax import lax
from jax.experimental import pallas as pl
from jax.experimental.pallas import tpu as pltpu
from jax.sharding import PartitionSpec as P

REL_MAX = 32
norm_eps = 1e-05
count_eps = 0.001
masked_score = -1000000000.0
LOG2E = 1.4426950408889634
MESH = pl.DeviceIdType.MESH
BF = jnp.bfloat16
F32 = jnp.float32

NR, NC = 16, 8
ND = NR * NC
SQ, RB, CB = 16, 44, 88
N = 704
RP = 48
WR = 2816 + 128
WL = 1408 + 128
S_R, S_L, S_QK, S_MK, S_B, S_T, S_G, S_X = range(8)


def norm(v):
    v = v.astype(F32)
    v = v - jnp.mean(v, axis=-1, keepdims=True)
    return v * lax.rsqrt(jnp.mean(v * v, axis=-1, keepdims=True) + norm_eps)


def dot(a, b):
    return jnp.dot(a, b, preferred_element_type=F32)


def dot_nt(a, b):
    return lax.dot_general(a, b, (((1,), (1,)), ((), ())), preferred_element_type=F32)


def dot_tn(a, b):
    return lax.dot_general(a, b, (((0,), (0,)), ((), ())), preferred_element_type=F32)


def iota(shape, dim):
    return lax.broadcasted_iota(jnp.int32, shape, dim)


def loop(low, high, body):
    def step(k, carry):
        body(k)
        return carry

    lax.fori_loop(low, high, step, 0)


def kernel(
    x_ref, pair_ref, mr_ref, ml_ref, scal_ref, colv_ref, live_ref, w_cov, w_q, w_kv, w_gate, w_mix,
    w_opm, dist_ref, w_all, w_valve, w_exit,
    out_a, out_b,
    zs0, zs1, zb, lhs_r, wbd_r, wbd_l, rmsg, lmsg, qmsg, bd, rt, xs, xb, acc_ref, zscr, hb, st_l, st_r,
    st_b, bmsg, tmsg, kf, kb, vb, biasbuf, gmsg, tout,
    rall, lall, qrecv, mrecv, brecv, trecv, grecv, xrecv,
    ssem, rsem,
):
    r = lax.axis_index("row")
    c = lax.axis_index("col")
    me = r * NC + c
    own = (r // 2) == c

    def send(src, dst, kind, rr, cc):
        pltpu.make_async_remote_copy(
            src, dst, ssem.at[kind], rsem.at[kind], device_id=(rr, cc), device_id_type=MESH
        ).start()

    def keep(src, dst, kind):
        pltpu.make_async_copy(src, dst, rsem.at[kind]).start()

    def arrived(ref, kind):
        pltpu.make_async_copy(ref, ref, rsem.at[kind]).wait()

    def sent(ref, kind):
        pltpu.make_async_copy(ref, ref, ssem.at[kind]).wait()

    bar = pltpu.get_barrier_semaphore()

    @pl.loop(1, ND)
    def _(k):
        pl.semaphore_signal(bar, inc=1, device_id=(r ^ (k // NC), c ^ (k % NC)), device_id_type=MESH)

    def msa_norm(s):
        v = norm(x_ref[s])
        at = pl.ds(pl.multiple_of(s * CB, 8), CB)
        zs0[at, :] = v[:, :128]
        zs1[at, :] = v[:, 128:]
        zb[s] = v.astype(BF)

    loop(0, SQ, msa_norm)

    cov = w_cov[...]
    for j in range(8):
        pick = (iota((32, 256), 1) == 8 * iota((32, 256), 0) + j).astype(BF)
        wbd_r[256 * j : 256 * j + 256, :] = dot(cov[:, 32:], pick).astype(BF)
    for j in range(4):
        pick = (iota((32, 128), 1) == 32 * j + iota((32, 128), 0)).astype(BF)
        wbd_l[256 * j : 256 * j + 256, :] = dot(cov[:, :32], pick).astype(BF)
    marks = mr_ref[...].astype(F32)
    for j in range(CB):
        g, b = j // 8, j % 8
        m = jnp.broadcast_to(marks[:, j : j + 1], (SQ, 128))
        lhs_r[16 * g : 16 * g + 16, 256 * b : 256 * b + 128] = (zs0[pl.ds(j, SQ, stride=CB), :] * m).astype(BF)
        lhs_r[16 * g : 16 * g + 16, 256 * b + 128 : 256 * b + 256] = (
            zs1[pl.ds(j, SQ, stride=CB), :] * m
        ).astype(BF)
    y = dot(lhs_r[...], wbd_r[...]).astype(BF)
    for g in range(11):
        rmsg[:, 256 * g : 256 * g + 256] = y[16 * g : 16 * g + 16]
    for b in range(2):
        y = dot(lhs_r[:, 1024 * b : 1024 * b + 1024], wbd_l[...]).astype(BF)
        for jg in range(11):
            g = 2 * jg + b
            lmsg[g // 11, :, 128 * (g % 11) : 128 * (g % 11) + 128] = y[16 * jg : 16 * jg + 16]
    rmsg[:, 2816:] = mr_ref[...]
    lmsg[0, :, 1408:] = ml_ref[0]
    lmsg[1, :, 1408:] = ml_ref[1]

    pl.semaphore_wait(bar, ND - 1)

    keep(rmsg, rall.at[r], S_R)
    for k in range(1, NR):
        send(rmsg, rall.at[r], S_R, r ^ k, c)
    for h in range(2):
        for b in range(NC):
            here = jnp.logical_and(own, jnp.logical_and(r % 2 == h, c == b))

            @pl.when(here)
            def _():
                keep(lmsg.at[h], lall.at[r], S_L)

            @pl.when(jnp.logical_not(here))
            def _():
                send(lmsg.at[h], lall.at[r], S_L, 2 * c + h, jnp.int32(b))

    scale = LOG2E / math.sqrt(32.0)

    def project(sg):
        ys = []
        for t in range(4):
            v = zb[4 * sg + t]
            kv = dot(v, w_kv[...])
            ys.append((dot(v, w_q[...]) * scale, kv[:, :256], kv[:, 256:], dot(v, w_gate[...])))
        for kind in range(4):
            for h in range(8):
                piece = jnp.concatenate([y[kind][:, 32 * h : 32 * h + 32] for y in ys], axis=1)
                qmsg[h, sg, :, 128 * kind : 128 * kind + 128] = piece.astype(BF)

    loop(0, 4, project)
    keep(qmsg.at[c], qrecv.at[c], S_QK)
    keep(mr_ref, mrecv.at[c], S_MK)
    for k in range(1, NC):
        send(mr_ref, mrecv.at[c], S_MK, r, c ^ k)
        send(qmsg.at[c ^ k], qrecv.at[c], S_QK, r, c ^ k)

    bd[...] = jnp.zeros_like(bd)

    arrived(rall, S_R)
    arrived(lall, S_L)
    for g in range(22):
        rt[128 * g : 128 * g + 128, :] = rall[:, :, 128 * g : 128 * g + 128].reshape(256, 128).T
    counts = dot_tn(
        rall[:, :, 2816:].reshape(256, 128), lall[:, :, 1408:].reshape(256, 128)
    ).astype(BF)
    for ig in range(6):
        lhs = lall[:, :, 256 * ig : 256 * ig + 256].reshape(256, 256)
        for part in range(4):
            at = slice(N * part, N * part + N)
            xs[at, :] = dot(rt[at, :], lhs)

        def regroup(e):
            rows = [xs[pl.ds(pl.multiple_of(256 * g + 8 * e, 8), 8), :] for g in range(11)]
            rows.append(jnp.zeros((8, 256), F32))
            xb[e, 96 * ig : 96 * ig + 96, :] = jnp.concatenate(rows, axis=0).astype(BF)

        loop(0, 32, regroup)

    for ec in range(4):
        for e in range(8):
            for i in range(8):
                bd[256 * e + 32 * i : 256 * e + 32 * i + 32, 128 * i : 128 * i + 128] = w_opm[8 * ec + e]
        for part in range(3):
            at = slice(192 * part, 192 * part + 192)
            lhs = jnp.concatenate([xb[8 * ec + e, at, :] for e in range(8)], axis=1)
            for n in range(4):
                y = dot(lhs, bd[:, 256 * n : 256 * n + 256])
                if ec:
                    acc_ref[at, 256 * n : 256 * n + 256] += y
                else:
                    acc_ref[at, 256 * n : 256 * n + 256] = y

    ordinals, strands = colv_ref[0], colv_ref[1]
    lane = iota((CB, 128), 1)
    fill = jnp.zeros((128 - CB, 128), F32)

    def wide(v):
        return jnp.concatenate([v, fill], axis=0).astype(BF)

    def pair_rows(ig, number):
        pick = (iota((128, 1024), 0) == 8 * ig + iota((128, 1024), 1) // 128).astype(BF)
        weight = 1.0 / (count_eps + dot(counts, pick)[:CB])
        rows = pl.ds(pl.multiple_of(96 * ig, 8), CB)
        for b in range(number):
            i = 8 * ig + b
            bins = jnp.clip(scal_ref[0, i] - ordinals + REL_MAX, 0, 2 * REL_MAX)
            bins = jnp.where(strands == scal_ref[1, i], bins, 2 * REL_MAX + 1)
            z = pair_ref[i].astype(F32) + dot((bins == lane).astype(BF), dist_ref[...])
            z = z + acc_ref[rows, 128 * b : 128 * b + 128] * weight[:, 128 * b : 128 * b + 128]
            zscr[i] = z
            v = norm(z)
            high = wide(v)
            low = (jnp.concatenate([v, fill], axis=0) - high.astype(F32)).astype(BF)
            hb[i] = high
            bias = dot_nt(w_all[512:528, :], high) + dot_nt(w_all[512:528, :], low)
            st_b[pl.ds(i, 8, stride=RP), :] = bias[:8] * LOG2E

    loop(0, 5, lambda ig: pair_rows(ig, 8))
    pair_rows(5, 4)

    for h in range(8):
        bmsg[h] = st_b[RP * h : RP * h + RP, :].astype(BF)
    keep(bmsg.at[c], brecv.at[me], S_B)

    @pl.loop(1, ND)
    def _(k):
        rr, cc = r ^ (k // NC), c ^ (k % NC)
        send(bmsg.at[cc], brecv.at[me], S_B, rr, cc)

    live = live_ref[...]

    def tri_rows(i):
        y = dot_nt(w_all[:512, :], hb[i])
        alive = live * scal_ref[2, i].astype(F32)
        st_l[pl.ds(i, 128, stride=RP), :] = jax.nn.sigmoid(y[128:256]) * y[:128] * alive
        st_r[pl.ds(i, 128, stride=RP), :] = jax.nn.sigmoid(y[384:]) * y[256:384] * alive

    loop(0, RB, tri_rows)

    def tri_pack(ch):
        at = pl.ds(pl.multiple_of(RP * ch, 8), RP)
        tmsg[ch, 0] = st_l[at, :].astype(BF)
        tmsg[ch, 1] = st_r[at, :].astype(BF)

    loop(0, ND, tri_pack)
    keep(tmsg.at[me], trecv.at[me], S_T)

    @pl.loop(1, ND)
    def _(k):
        rr, cc = r ^ (k // NC), c ^ (k % NC)
        send(tmsg.at[rr * NC + cc], trecv.at[me], S_T, rr, cc)

    arrived(qrecv, S_QK)
    arrived(mrecv, S_MK)

    def gather_keys(sg):
        for b in range(NC):
            kf[CB * b : CB * b + CB, :] = qrecv[b, sg, :, 128:256].astype(F32)
        kb[sg] = kf[...].astype(BF)
        for b in range(NC):
            kf[CB * b : CB * b + CB, :] = qrecv[b, sg, :, 256:384].astype(F32)
        vb[sg, :, :128] = kf[...].astype(BF)
        vb[sg, :, 128:] = jnp.ones((N, 128), BF)

    loop(0, 4, gather_keys)
    every = jnp.concatenate([mrecv[b].astype(F32)[:, :CB] for b in range(NC)], axis=1)
    madd = jnp.where(every > 0, 0.0, masked_score)
    group = lane // 32
    arrived(brecv, S_B)

    def attend(k):
        cb = c ^ k
        halves = []
        for d in range(2):
            row = [brecv[(2 * cb + d) * NC + b].astype(F32)[:RB, :CB] for b in range(NC)]
            halves.append(jnp.concatenate(row, axis=1))
        biasbuf[...] = jnp.concatenate(halves, axis=0)
        for sg in range(4):
            own_q = qrecv[cb, sg].astype(F32)
            q = jnp.concatenate([jnp.where(group == t, own_q[:, :128], 0.0) for t in range(4)], axis=0)
            s = dot_nt(q.astype(BF), kb[sg])
            ps = []
            for t in range(4):
                v = s[CB * t : CB * t + CB] + biasbuf[...] + madd[4 * sg + t : 4 * sg + t + 1]
                ps.append(jnp.exp2(v - jnp.max(v, axis=-1, keepdims=True)))
            o = dot(jnp.concatenate(ps, axis=0).astype(BF), vb[sg])
            o = o[:, :128] / o[:, 128:]
            mixed = o[:CB]
            for t in range(1, 4):
                mixed = jnp.where(group == t, o[CB * t : CB * t + CB], mixed)
            gmsg[cb, sg] = (jax.nn.sigmoid(own_q[:, 384:]) * mixed).astype(BF)

        @pl.when(k == 0)
        def _():
            keep(gmsg.at[c], grecv.at[c], S_G)

        @pl.when(k > 0)
        def _():
            send(gmsg.at[cb], grecv.at[c], S_G, r, cb)

    loop(0, NC, attend)

    arrived(trecv, S_T)
    for pair in range(4):
        total = None
        for b in range(0, NC, 2):
            lhs, rhs = [], []
            for d in range(2):
                lhs.append(jnp.concatenate([trecv[q * NC + b + d, 0] for q in range(NR)], axis=0))
                rhs.append(jnp.concatenate([trecv[(4 * pair + q) * NC + b + d, 1] for q in range(4)], axis=0))
            y = dot_nt(jnp.concatenate(lhs, axis=1), jnp.concatenate(rhs, axis=1))
            total = y if total is None else total + y
        for h in range(2):
            at = 96 * h
            row = jnp.concatenate(
                [total[:, at : at + RB], total[:, at + RP : at + RP + RB], jnp.zeros((NR * RP, 128 - CB), F32)],
                axis=1,
            ).astype(BF)
            for q in range(NR):
                tout[q * NC + 2 * pair + h] = row[RP * q : RP * q + RP]

        @pl.loop(0, 2 * NR)
        def _(k):
            rr, cc = r ^ (k // 2), 2 * pair + k % 2
            here = jnp.logical_and(rr == r, cc == c)

            @pl.when(here)
            def _():
                keep(tout.at[me], xrecv.at[me], S_X)

            @pl.when(jnp.logical_not(here))
            def _():
                send(tout.at[rr * NC + cc], xrecv.at[me], S_X, rr, cc)

    arrived(grecv, S_G)
    w_rep = []
    for h in range(8):
        w_rep += [w_mix[32 * h : 32 * h + 32, :]] * 4
    w_rep = jnp.concatenate(w_rep, axis=0)
    wide_group = iota((CB, 1024), 1) % 128 // 32

    def mix(sg):
        cat = jnp.concatenate([grecv[h, sg].astype(F32) for h in range(8)], axis=1)
        for t in range(4):
            y = dot(jnp.where(wide_group == t, cat, 0.0).astype(BF), w_rep)
            out_a[4 * sg + t] = (x_ref[4 * sg + t].astype(F32) + y).astype(BF)

    loop(0, 4, mix)

    arrived(xrecv, S_X)
    for part in range(3):
        rows = slice(16 * part, 16 * part + 16)
        total = lax.fori_loop(
            0, ND, lambda ch, t: t + xrecv[ch, rows, :].astype(F32), jnp.zeros((16, 128), F32)
        )
        mean = total * (1.0 / 128)

        def square(ch, t):
            d = xrecv[ch, rows, :].astype(F32) - mean
            return t + d * d

        total = lax.fori_loop(0, ND, square, jnp.zeros((16, 128), F32))
        inv = lax.rsqrt(total * (1.0 / 128) + norm_eps)

        def scaled(ch):
            at = pl.ds(pl.multiple_of(RP * ch + 16 * part, 8), 16)
            st_l[at, :] = (xrecv[ch, rows, :].astype(F32) - mean) * inv

        loop(0, ND, scaled)

    def last(i):
        cross = st_l[pl.ds(i, 128, stride=RP), :].astype(BF)
        proj = dot_tn(cross, w_exit[...])[:CB]
        gate = jax.nn.sigmoid(dot(hb[i], w_valve[...])[:CB])
        out_b[i] = (zscr[i] + gate * proj).astype(BF)

    loop(0, RB, last)

    sent(rall.at[pl.ds(0, NR - 1)], S_R)

    @pl.when(own)
    def _():
        sent(lall.at[pl.ds(0, NR - 1)], S_L)

    @pl.when(jnp.logical_not(own))
    def _():
        sent(lall, S_L)

    sent(qrecv.at[pl.ds(0, NC - 1)], S_QK)
    sent(mrecv.at[pl.ds(0, NC - 1)], S_MK)
    sent(brecv.at[pl.ds(0, ND - 1)], S_B)
    sent(trecv.at[pl.ds(0, ND - 1)], S_T)
    sent(grecv.at[pl.ds(0, NC - 1)], S_G)
    sent(xrecv.at[pl.ds(0, ND - 1)], S_X)


def run(*operands):
    vm = pl.BlockSpec(memory_space=pltpu.VMEM)
    sm = pl.BlockSpec(memory_space=pltpu.SMEM)
    V = pltpu.VMEM
    scratch = [
        V((SQ * CB, 128), F32), V((SQ * CB, 128), F32), V((SQ, CB, 256), BF),
        V((176, 2048), BF), V((2048, 256), BF), V((1024, 128), BF),
        V((SQ, WR), BF), V((2, SQ, WL), BF), V((8, 4, CB, 512), BF),
        V((2048, 1024), BF), V((2816, 256), BF), V((2816, 256), F32),
        V((32, 576, 256), BF), V((576, 1024), F32),
        V((RB, CB, 128), F32), V((RB, 128, 128), BF),
        V((ND * RP, 128), F32), V((ND * RP, 128), F32), V((8 * RP, 128), F32),
        V((8, RP, 128), BF), V((ND, 2, RP, 128), BF),
        V((N, 128), F32), V((4, N, 128), BF), V((4, N, 256), BF), V((CB, N), F32),
        V((NC, 4, CB, 128), BF), V((ND, RP, 128), BF),
        V((NR, SQ, WR), BF), V((NR, SQ, WL), BF), V((NC, 4, CB, 512), BF), V((NC, SQ, 128), BF),
        V((ND, RP, 128), BF), V((ND, 2, RP, 128), BF), V((NC, 4, CB, 128), BF), V((ND, RP, 128), BF),
        pltpu.SemaphoreType.DMA((8,)), pltpu.SemaphoreType.DMA((8,)),
    ]
    return pl.pallas_call(
        kernel,
        out_shape=(
            jax.ShapeDtypeStruct((SQ, CB, 256), BF),
            jax.ShapeDtypeStruct((RB, CB, 128), BF),
        ),
        in_specs=[vm] * 4 + [sm] + [vm] * 12,
        out_specs=(vm, vm),
        scratch_shapes=scratch,
        compiler_params=pltpu.CompilerParams(
            collective_id=0, has_side_effects=True, vmem_limit_bytes=63 << 20
        ),
    )(*operands)


def shards(
    msa, pair, marks, res_marks, ordinals, strand, dist_vectors, w_bias, w_q, w_kv, w_gate, w_mix,
    w_cov, w_opm, w_tri, w_valve, w_exit,
):
    r = lax.axis_index("row")
    c = lax.axis_index("col")
    marks_b = marks.astype(BF)
    mr = jnp.pad(marks_b, ((0, 0), (0, 128 - CB)))
    ml = jnp.stack([jnp.pad(marks_b[:, RB * h : RB * h + RB], ((0, 0), (0, 128 - RB))) for h in range(2)])
    three = jnp.stack([ordinals, strand, res_marks])
    scal = lax.dynamic_slice_in_dim(three, r * RB, RB, 1)
    cols = lax.dynamic_slice_in_dim(three, c * CB, CB, 1)
    colv = jnp.broadcast_to(cols[:2, :, None], (2, CB, 128))
    live = jnp.pad(cols[2:].astype(F32), ((0, 0), (0, 128 - CB)))
    w_opm_e = w_opm.reshape(32, 32, 128).swapaxes(0, 1)
    dist = jnp.pad(dist_vectors, ((0, 128 - dist_vectors.shape[0]), (0, 0)))
    w_all = jnp.concatenate([w_tri.T, jnp.pad(w_bias.T, ((0, 8), (0, 0)))], axis=0)
    return run(
        msa, pair, mr, ml, scal, colv, live, w_cov, w_q, w_kv, w_gate, w_mix, w_opm_e, dist, w_all,
        w_valve, w_exit,
    )


def solution(mesh):
    placed = (P("row", "col", None), P("row", "col", None), P("row", "col")) + (P(),) * 14
    return jax.shard_map(
        shards,
        mesh=mesh,
        in_specs=placed,
        out_specs=(P("row", "col", None), P("row", "col", None)),
        check_vma=False,
    )
```

time: 366 us -> 219 us (0.60); the launches traced: 361 us -> 218 us
  blocking collectives: 101 us -> 0 us
  Pallas kernels: 112 us -> 207 us
  waiting for transfers between devices: 43.2 us -> 0 us
  matrix products: 33.9 us -> 0 us
  starting transfers between devices: 26.6 us -> 0 us
  local copies, waits for them, and re-layouts: 30.3 us -> 9.7 us
  other arithmetic: 13 us -> 1.28 us
    pallas_call x4 -> x1, Pallas kernels: 112 us -> 207 us  [run(): pl.pallas_call(kernel, out_shape=(jax.ShapeDtypeStruct((SQ, CB, 256), BF)...]
    all_gather x2 -> x0, blocking collectives: 90 us -> none  [the longest x1 63.9 us: shards(): every_marks = lax.all_gather(marks, 'col', axis=1, tiled=True)]
    all_to_all x4 -> x0, waiting for transfers between devices: 43.2 us -> none  [the longest x1 19.7 us: shards(): qk = lax.all_to_all(qk, 'col', 0, 0, tiled=True)]
    dot_general x8 -> x0, matrix products: 33.9 us -> none  [the longest x4 16.4 us: dot(): return jnp.dot(a, b, preferred_element_type=F32)]
    all_to_all x4 -> x0, starting transfers between devices: 26.6 us -> none  [the longest x1 7.64 us: shards(): lax.all_to_all(crossed.reshape(128, RP, 128), ('row', 'col'), 0, 0, tiled...]
    all_to_all x1 -> x0, blocking collectives: 11.2 us -> none  [shards(): bias = lax.all_to_all(bias, 'col', 0, 0, tiled=True)]
    unnamed x51 -> x26, local copies, waits for them, and re-layouts: 13.4 us -> 5.54 us
    reduce_sum x3 -> x0, other arithmetic: 5.1 us -> none  [the longest x1 1.96 us: shards(): jnp.mean(crossed * crossed, axis=0, keepdims=True) + norm_eps]
  transfers between devices with their start and end apart: 4 -> 0, of which waited for: 3 -> 0; matrix products, arithmetic and copies ran while one was open for 7% -> 0% of each run, Pallas kernels for 15% -> 0%
where the time goes in v2:
time: 219 us; the launch traced here: 218 us
  Pallas kernels  207 us (95%)
  local copies, waits for them, and re-layouts  9.7 us (4%)
    pallas_call x1, Pallas kernels, run(): pl.pallas_call(kernel, out_shape=(jax.ShapeDtypeStruct((SQ, CB, 256), BF)...  207 us
    unnamed x26, local copies, waits for them, and re-layouts  5.54 us

profile of v2, /device:TPU:96, one launch (start us, length us, event | category | flops | bytes accessed | tf_op | source)
XLA Modules:
  0.0 218.4 jit_solution(380684888074470357)
XLA Ops:
  0.6 0.0 copy-start.7
  0.6 0.0 copy-start.8
  0.7 0.7 copy-done.7
  1.3 0.0 copy-done.8
  1.3 0.0 copy-start.9
  1.3 0.7 copy-done.9
  2.0 0.0 copy-start.5
  2.1 0.1 constant_dynamic-slice_fusion
  2.1 0.0 copy-start.6
  2.1 0.7 constant_dynamic-slice_fusion.1.scal_ref
  2.8 0.0 copy-done.6
  2.8 0.6 pad.26.live_ref
  3.4 0.0 copy-done.5
  3.4 0.6 pad.23.mr_ref
  4.0 0.1 fusion.2
  4.1 0.0 copy-start.4
  4.1 0.0 copy-start.3
  4.1 0.0 copy-start.2
  4.1 0.6 pad_maximum_fusion.ml_ref
  4.7 0.1 copy-done.4
  4.8 0.6 pad.27.dist_ref
  5.4 0.0 copy-done.3
  5.4 0.0 slice-start
  5.4 0.7 copy.23.w_cov
  6.1 0.0 slice-done
  6.1 0.0 copy-start.10
  6.2 0.7 broadcast_in_dim.2.colv_ref
  6.9 0.0 copy-done.2
  6.9 0.0 copy-start.1
  6.9 0.1 copy.22
  7.0 0.0 copy-done.10
  7.0 0.7 fusion.1.w_all
  7.7 0.1 copy-done.1
  7.8 0.8 copy.25
  8.6 206.6 %shard_map.176 = (bf16[16,88,256]{2,1,0:T(8,128)(2,1)}, bf16[44,88,128]{2,1,0:T(8,128)(2,1)}) custom-call(bf16[16,88,256]{2,1,0:T(8,128)(2,1)} %x_ref.1, bf16[44,88,128]{2,1,0:T(8,128)(2,1)} %pair_ref.1, bf16[16,128]{1,0:T(8,128)(2,1)} %pad.23.mr_ref, bf16[2,16,128]{2,1,0:T(8,128)(2,1)} %pad_maximum_fusion.ml_ref, ...), custom_call_target="tpu_custom_call" | custom-call | tf_op jit(solution)/shard_map/pallas_call | solution.py:425
  215.3 0.0 copy-start
  215.3 2.1 copy.28
  217.4 0.0 copy-done
  217.4 0.9 copy.29
  (7 shorter events, 0.0 us)
Async XLA Ops:
  0.6 0.7 copy-start.7
  0.6 0.7 copy-start.8
  1.3 0.7 copy-start.9
  2.0 1.3 copy-start.5
  2.1 0.7 copy-start.6
  4.1 0.7 copy-start.4
  4.1 1.3 copy-start.3
  4.1 2.8 %copy-start.2 = (bf16[128,512]{1,0:T(8,128)(2,1)S(1)}, bf16[128,512]{1,0:T(8,128)(2,1)}, u32[]{:S(2)}) copy-start(bf16[128,512]{1,0:T(8,128)(2,1)} %param.31) | copy-start | bytes 393220
  5.4 0.7 slice-start
  6.1 0.9 copy-start.10
  6.9 1.0 copy-start.1
  215.3 2.1 copy-start

commit v3 on v2

v3 whole, which is shorter than its diff:
```python
import math

import jax
import jax.numpy as jnp
from jax import lax
from jax.experimental import pallas as pl
from jax.experimental.pallas import tpu as pltpu
from jax.sharding import PartitionSpec as P

REL_MAX = 32
norm_eps = 1e-05
count_eps = 0.001
masked_score = -1000000000.0
LOG2E = 1.4426950408889634
MESH = pl.DeviceIdType.MESH
BF = jnp.bfloat16
F32 = jnp.float32

NR, NC = 16, 8
ND = NR * NC
SQ, RB, CB = 16, 44, 88
N = 704
RP = 48
WR = 2816 + 128
WL = 1408 + 128
S_R, S_R2, S_L, S_QK, S_MK, S_B, S_B2, S_TL, S_TR, S_G, S_X = range(11)
PK = 32


def norm(v):
    v = v.astype(F32)
    v = v - jnp.mean(v, axis=-1, keepdims=True)
    return v * lax.rsqrt(jnp.mean(v * v, axis=-1, keepdims=True) + norm_eps)


def dot(a, b):
    return jnp.dot(a, b, preferred_element_type=F32)


def dot_nt(a, b):
    return lax.dot_general(a, b, (((1,), (1,)), ((), ())), preferred_element_type=F32)


def dot_tn(a, b):
    return lax.dot_general(a, b, (((0,), (0,)), ((), ())), preferred_element_type=F32)


def iota(shape, dim):
    return lax.broadcasted_iota(jnp.int32, shape, dim)


def loop(low, high, body, unroll=1):
    def step(k, carry):
        body(k)
        return carry

    lax.fori_loop(low, high, step, 0, unroll=unroll)


def roll(v, lanes):
    return pltpu.roll(v, lanes, 1)


def pack(u):
    lane, sub = iota((8, 128), 1), iota((8, 128), 0)
    extra = (
        roll(u[4], 88),
        roll(u[4], 48),
        jnp.where(sub < 4, roll(u[5], 88), pltpu.roll(roll(u[5], 48), 4, 0)),
        jnp.where(lane < 96, roll(u[4], 8), roll(u[5], 16)),
    )
    return jnp.concatenate([jnp.where(lane < CB, u[k], extra[k]) for k in range(4)], axis=0)


def unpack(p):
    lane = iota((8, 128), 1)
    p = [p[8 * k : 8 * k + 8] for k in range(4)]
    low, mid, high = lane < 40, lane < 80, lane < CB
    u = [jnp.where(high, v, 0.0) for v in p]
    tail = jnp.where(high, roll(p[3], 120), 0.0)
    u.append(jnp.where(low, roll(p[0], 40), jnp.where(mid, roll(p[1], 80), tail)))
    tail = jnp.where(high, roll(p[3], 112), 0.0)
    u.append(jnp.where(low, roll(p[2], 40), jnp.where(mid, pltpu.roll(roll(p[2], 80), 4, 0), tail)))
    return u


def kernel(
    x_ref, pair_ref, marks_ref, code_ref, code_col, w_cov, w_q, w_kv, w_gate, w_mix,
    w_opm, dist_ref, w_tri, w_bias, w_valve, w_exit,
    out_a, out_b,
    zs0, zs1, zb, lhs_r, wbd_r, wbd_l, w_all, w_opm_e, gates, mmsg, rmsg, lmsg, qmsg, bd, rt, xs, xb, acc_ref,
    zscr, hb, st, st_b, bmsg, tl_msg, tr_msg, kf, kb, vb, biasbuf, gmsg, lbuf, rbuf, pbuf, tout, stats,
    rall, lall, qrecv, mrecv, brecv, tl_recv, tr_recv, grecv, xrecv,
    ssem, rsem,
):
    r = lax.axis_index("row")
    c = lax.axis_index("col")
    me = r * NC + c
    own = (r // 2) == c

    def send(src, dst, kind, rr, cc):
        pltpu.make_async_remote_copy(
            src, dst, ssem.at[kind], rsem.at[kind], device_id=(rr, cc), device_id_type=MESH
        ).start()

    def keep(src, dst, kind):
        pltpu.make_async_copy(src, dst, rsem.at[kind]).start()

    def arrived(ref, kind):
        pltpu.make_async_copy(ref, ref, rsem.at[kind]).wait()

    def sent(ref, kind):
        pltpu.make_async_copy(ref, ref, ssem.at[kind]).wait()

    bar = pltpu.get_barrier_semaphore()

    @pl.loop(1, ND)
    def _(k):
        pl.semaphore_signal(bar, inc=1, device_id=(r ^ (k // NC), c ^ (k % NC)), device_id_type=MESH)

    for k in range(4):
        w_all[128 * k : 128 * k + 128, :] = w_tri[:, 128 * k : 128 * k + 128].T
    w_all[512:, :] = jnp.concatenate([w_bias[...].astype(F32), jnp.zeros((8, 128), F32)], axis=0).astype(BF)

    def msa_norm(s):
        v = norm(x_ref[s])
        at = pl.ds(pl.multiple_of(s * CB, 8), CB)
        zs0[at, :] = v[:, :128]
        zs1[at, :] = v[:, 128:]
        zb[s] = v.astype(BF)

    loop(0, SQ, msa_norm)

    cov = w_cov[...]
    for j in range(8):
        pick = (iota((32, 256), 1) == 8 * iota((32, 256), 0) + j).astype(BF)
        wbd_r[256 * j : 256 * j + 256, :] = dot_tn(cov[32:], pick).astype(BF)
    for j in range(4):
        pick = (iota((32, 128), 1) == 32 * j + iota((32, 128), 0)).astype(BF)
        wbd_l[256 * j : 256 * j + 256, :] = dot_tn(cov[:32], pick).astype(BF)
    marks = marks_ref[...].astype(F32)
    mmsg[...] = jnp.concatenate([marks, jnp.zeros((SQ, 128 - CB), F32)], axis=1).astype(BF)
    for j in range(CB):
        g, b = j // 8, j % 8
        m = jnp.broadcast_to(marks[:, j : j + 1], (SQ, 128))
        lhs_r[16 * g : 16 * g + 16, 256 * b : 256 * b + 128] = (zs0[pl.ds(j, SQ, stride=CB), :] * m).astype(BF)
        lhs_r[16 * g : 16 * g + 16, 256 * b + 128 : 256 * b + 256] = (
            zs1[pl.ds(j, SQ, stride=CB), :] * m
        ).astype(BF)
    y = dot(lhs_r[...], wbd_r[...]).astype(BF)
    for g in range(11):
        rmsg[:, 256 * g : 256 * g + 256] = y[16 * g : 16 * g + 16]
    for b in range(2):
        y = dot(lhs_r[:, 1024 * b : 1024 * b + 1024], wbd_l[...]).astype(BF)
        for jg in range(11):
            g = 2 * jg + b
            lmsg[g // 11, :, 128 * (g % 11) : 128 * (g % 11) + 128] = y[16 * jg : 16 * jg + 16]
    rmsg[:, 2816:] = mmsg[...]
    for h in range(2):
        part = [marks[:, RB * h : RB * h + RB], jnp.zeros((SQ, 128 - RB), F32)]
        lmsg[h, :, 1408:] = jnp.concatenate(part, axis=1).astype(BF)

    pl.semaphore_wait(bar, ND - 1)

    keep(rmsg, rall.at[r], S_R)
    for k in range(2, NR, 2):
        send(rmsg, rall.at[r], S_R, r ^ k, c)
    send(rmsg, rall.at[r], S_R2, r ^ 1, c)
    for h in range(2):
        for b in range(NC):
            here = jnp.logical_and(own, jnp.logical_and(r % 2 == h, c == b))

            @pl.when(here)
            def _():
                keep(lmsg.at[h], lall.at[r], S_L)

            @pl.when(jnp.logical_not(here))
            def _():
                send(lmsg.at[h], lall.at[r], S_L, 2 * c + h, jnp.int32(b))

    scale = LOG2E / math.sqrt(32.0)

    w_wide = []
    for h in range(8):
        w_wide += [w_gate[:, 32 * h : 32 * h + 32]] * 4
    w_wide = jnp.concatenate(w_wide, axis=1)
    wide_group = iota((CB, 1024), 1) % 128 // 32

    def project(sg):
        ys = []
        gate = None
        for t in range(4):
            v = zb[4 * sg + t]
            kv = dot(v, w_kv[...])
            ys.append((dot(v, w_q[...]) * scale, kv[:, :256], kv[:, 256:]))
            y = dot(v, w_wide)
            gate = y if gate is None else jnp.where(wide_group == t, y, gate)
        gates[sg] = jax.nn.sigmoid(gate)
        for kind in range(3):
            for h in range(8):
                piece = jnp.concatenate([y[kind][:, 32 * h : 32 * h + 32] for y in ys], axis=1)
                qmsg[h, sg, :, 128 * kind : 128 * kind + 128] = piece.astype(BF)

    loop(0, 4, project)

    bd[...] = jnp.zeros_like(bd)
    st[0:1024, :] = w_opm[...].astype(F32)
    for e in range(32):
        w_opm_e[e] = st[pl.ds(e, 32, stride=32), :].astype(BF)

    arrived(rall.at[pl.ds(0, 8)], S_R)
    for k in range(2, NR, 2):
        send(rall.at[r ^ k], rall.at[r ^ k], S_R2, r ^ 1, c)
    arrived(lall, S_L)
    arrived(rall.at[pl.ds(0, 8)], S_R2)

    keep(qmsg.at[c], qrecv.at[c], S_QK)
    keep(mmsg, mrecv.at[c], S_MK)
    for k in range(1, NC):
        send(mmsg, mrecv.at[c], S_MK, r, c ^ k)
        send(qmsg.at[c ^ k], qrecv.at[c], S_QK, r, c ^ k)

    for g in range(22):
        rt[128 * g : 128 * g + 128, :] = rall[:, :, 128 * g : 128 * g + 128].reshape(256, 128).T
    counts = dot_tn(
        rall[:, :, 2816:].reshape(256, 128), lall[:, :, 1408:].reshape(256, 128)
    ).astype(BF)
    for ig in range(6):
        lhs = lall[:, :, 256 * ig : 256 * ig + 256].reshape(256, 256)
        for part in range(4):
            at = slice(N * part, N * part + N)
            xs[at, :] = dot(rt[at, :], lhs)

        def regroup(e):
            rows = [xs[pl.ds(pl.multiple_of(256 * g + 8 * e, 8), 8), :] for g in range(11)]
            rows.append(jnp.zeros((8, 256), F32))
            xb[e, 96 * ig : 96 * ig + 96, :] = jnp.concatenate(rows, axis=0).astype(BF)

        loop(0, 32, regroup)

    for ec in range(4):
        for e in range(8):
            for i in range(8):
                bd[256 * e + 32 * i : 256 * e + 32 * i + 32, 128 * i : 128 * i + 128] = w_opm_e[8 * ec + e]
        for part in range(3):
            at = slice(192 * part, 192 * part + 192)
            lhs = jnp.concatenate([xb[8 * ec + e, at, :] for e in range(8)], axis=1)
            for n in range(4):
                y = dot(lhs, bd[:, 256 * n : 256 * n + 256])
                if ec:
                    acc_ref[at, 256 * n : 256 * n + 256] += y
                else:
                    acc_ref[at, 256 * n : 256 * n + 256] = y

    code = code_col[...]
    ordinals, strands = code % 4096, code // 4096 % 16
    lane = iota((CB, 128), 1)
    kind = iota((CB, dist_ref.shape[0]), 1)
    ordinals, strands = ordinals[:, : kind.shape[1]], strands[:, : kind.shape[1]]
    fill = jnp.zeros((128 - CB, 128), F32)

    def wide(v):
        return jnp.concatenate([v, fill], axis=0).astype(BF)

    def pair_rows(ig, number):
        pick = (iota((128, 1024), 0) == 8 * ig + iota((128, 1024), 1) // 128).astype(BF)
        weight = 1.0 / (count_eps + dot(counts, pick)[:CB])
        rows = pl.ds(pl.multiple_of(96 * ig, 8), CB)
        for b in range(number):
            i = 8 * ig + b
            row_code = code_ref[r * RB + i]
            bins = jnp.clip(row_code % 4096 - ordinals + REL_MAX, 0, 2 * REL_MAX)
            bins = jnp.where(strands == row_code // 4096 % 16, bins, 2 * REL_MAX + 1)
            z = pair_ref[i].astype(F32) + dot((bins == kind).astype(BF), dist_ref[...])
            z = z + acc_ref[rows, 128 * b : 128 * b + 128] * weight[:, 128 * b : 128 * b + 128]
            zscr[i] = z
            v = norm(z)
            high = wide(v)
            low = (jnp.concatenate([v, fill], axis=0) - high.astype(F32)).astype(BF)
            hb[i] = high
            bias = dot_nt(w_all[512:528, :], high) + dot_nt(w_all[512:528, :], low)
            st_b[pl.ds(i, 8, stride=RP), :] = bias[:8] * LOG2E

    loop(0, 5, lambda ig: pair_rows(ig, 8))
    pair_rows(5, 4)

    def packed(ref, first):
        return pack([ref[pl.ds(pl.multiple_of(first + 8 * k, 8), 8), :] for k in range(6)]).astype(BF)

    for h in range(8):
        bmsg[h] = packed(st_b, RP * h)
    keep(bmsg.at[c], brecv.at[me], S_B)

    @pl.loop(1, ND // 2)
    def _(k):
        rr, cc = r ^ (k // NC * 2), c ^ (k % NC)
        send(bmsg.at[cc], brecv.at[me], S_B, rr, cc)

    live = jnp.concatenate([(code // 65536).astype(F32), fill], axis=0).T[:1]

    def tri_side(base, msg, recv, sem):
        def tri_rows(i):
            y = dot_nt(w_all[base : base + 256, :], hb[i])
            alive = live * (code_ref[r * RB + i] // 65536).astype(F32)
            st[pl.ds(i, 128, stride=RP), :] = jax.nn.sigmoid(y[128:]) * y[:128] * alive

        loop(0, RB, tri_rows, 2)

        def tri_pack(ch):
            msg[ch] = packed(st, RP * ch)

        loop(0, ND, tri_pack, 4)
        keep(msg.at[me], recv.at[me], sem)

        @pl.loop(1, ND)
        def _(k):
            rr, cc = r ^ (k // NC), c ^ (k % NC)
            send(msg.at[rr * NC + cc], recv.at[me], sem, rr, cc)

    tri_side(0, tl_msg, tl_recv, S_TL)

    arrived(brecv.at[pl.ds(0, ND // 2)], S_B)
    for k in range(0, NR, 2):
        at = pl.ds((r ^ k) * NC, NC)
        send(brecv.at[at], brecv.at[at], S_B2, r ^ 1, c)

    tri_side(256, tr_msg, tr_recv, S_TR)

    arrived(qrecv, S_QK)
    arrived(mrecv, S_MK)

    def gather_keys(sg):
        for b in range(NC):
            kf[CB * b : CB * b + CB, :] = qrecv[b, sg, :, 128:256].astype(F32)
        kb[sg] = kf[...].astype(BF)
        for b in range(NC):
            kf[CB * b : CB * b + CB, :] = qrecv[b, sg, :, 256:384].astype(F32)
        vb[sg, :, :128] = kf[...].astype(BF)
        vb[sg, :, 128:] = jnp.ones((N, 128), BF)

    loop(0, 4, gather_keys)
    every = jnp.concatenate([mrecv[b].astype(F32)[:, :CB] for b in range(NC)], axis=1)
    madd = jnp.where(every > 0, 0.0, masked_score)
    group = lane // 32
    arrived(brecv.at[pl.ds(0, ND // 2)], S_B2)

    def attend(k):
        cb = c ^ k
        halves = []
        for d in range(2):
            row = [
                jnp.concatenate(unpack(brecv[(2 * cb + d) * NC + b].astype(F32)), axis=0)[:RB, :CB]
                for b in range(NC)
            ]
            halves.append(jnp.concatenate(row, axis=1))
        biasbuf[...] = jnp.concatenate(halves, axis=0)
        for sg in range(4):
            own_q = qrecv[cb, sg].astype(F32)
            q = jnp.concatenate([jnp.where(group == t, own_q[:, :128], 0.0) for t in range(4)], axis=0)
            s = dot_nt(q.astype(BF), kb[sg])
            ps = []
            for t in range(4):
                v = s[CB * t : CB * t + CB] + biasbuf[...] + madd[4 * sg + t : 4 * sg + t + 1]
                ps.append(jnp.exp2(v - jnp.max(v, axis=-1, keepdims=True)))
            o = dot(jnp.concatenate(ps, axis=0).astype(BF), vb[sg])
            o = o[:, :128] / o[:, 128:]
            mixed = o[:CB]
            for t in range(1, 4):
                mixed = jnp.where(group == t, o[CB * t : CB * t + CB], mixed)
            gmsg[cb, sg] = mixed.astype(BF)

        @pl.when(k == 0)
        def _():
            keep(gmsg.at[c], grecv.at[c], S_G)

        @pl.when(k > 0)
        def _():
            send(gmsg.at[cb], grecv.at[c], S_G, r, cb)

    loop(0, NC, attend)

    def unpack_side(recv, buf):
        def step(q):
            for b in range(NC):
                tile = jnp.concatenate(unpack(recv[q * NC + b].astype(F32)), axis=0).astype(BF)
                buf[b // 2, pl.ds(pl.multiple_of(RP * q, 16), RP), 128 * (b % 2) : 128 * (b % 2) + 128] = tile

        loop(0, NR, step)

    arrived(tl_recv, S_TL)
    unpack_side(tl_recv, lbuf)
    arrived(tr_recv, S_TR)
    unpack_side(tr_recv, rbuf)
    for pair in range(4):
        total = None
        for b in range(4):
            y = dot_nt(lbuf[b], rbuf[b, 4 * RP * pair : 4 * RP * pair + 4 * RP, :])
            total = y if total is None else total + y
        for h in range(2):
            at = 96 * h
            pbuf[...] = jnp.concatenate(
                [total[:, at : at + RB], total[:, at + RP : at + RP + RB], jnp.zeros((NR * RP, 128 - CB), F32)],
                axis=1,
            )

            def cross_pack(q):
                tout[q * NC + 2 * pair + h] = packed(pbuf, RP * q)

            loop(0, NR, cross_pack, 4)

        @pl.loop(0, 2 * NR)
        def _(k):
            rr, cc = r ^ (k // 2), 2 * pair + k % 2
            here = jnp.logical_and(rr == r, cc == c)

            @pl.when(here)
            def _():
                keep(tout.at[me], xrecv.at[me], S_X)

            @pl.when(jnp.logical_not(here))
            def _():
                send(tout.at[rr * NC + cc], xrecv.at[me], S_X, rr, cc)

    arrived(grecv, S_G)
    w_rep = []
    for h in range(8):
        w_rep += [w_mix[32 * h : 32 * h + 32, :]] * 4
    w_rep = jnp.concatenate(w_rep, axis=0)

    def mix(sg):
        cat = jnp.concatenate([grecv[h, sg].astype(F32) for h in range(8)], axis=1) * gates[sg]
        for t in range(4):
            y = dot(jnp.where(wide_group == t, cat, 0.0).astype(BF), w_rep)
            out_a[4 * sg + t] = (x_ref[4 * sg + t].astype(F32) + y).astype(BF)

    loop(0, 4, mix)

    arrived(xrecv, S_X)

    def add(ch, t):
        u = jnp.concatenate(unpack(xrecv[ch].astype(F32)), axis=0)
        st[pl.ds(pl.multiple_of(RP * ch, 8), RP), :] = u
        return t + u

    mean = lax.fori_loop(0, ND, add, jnp.zeros((RP, 128), F32), unroll=4) * (1.0 / 128)

    def square(ch, t):
        d = st[pl.ds(pl.multiple_of(RP * ch, 8), RP), :] - mean
        return t + d * d

    total = lax.fori_loop(0, ND, square, jnp.zeros((RP, 128), F32), unroll=4)
    stats[0:RP, :] = mean
    stats[RP:, :] = lax.rsqrt(total * (1.0 / 128) + norm_eps)

    def last(i):
        cross = (st[pl.ds(i, 128, stride=RP), :] - stats[pl.ds(i, 1), :]) * stats[pl.ds(RP + i, 1), :]
        proj = dot_tn(cross.astype(BF), w_exit[...])[:CB]
        gate = jax.nn.sigmoid(dot(hb[i], w_valve[...])[:CB])
        out_b[i] = (zscr[i] + gate * proj).astype(BF)

    loop(0, RB, last, 2)

    sent(rall.at[pl.ds(0, 7)], S_R)
    sent(rall.at[pl.ds(0, 8)], S_R2)

    @pl.when(own)
    def _():
        sent(lall.at[pl.ds(0, NR - 1)], S_L)

    @pl.when(jnp.logical_not(own))
    def _():
        sent(lall, S_L)

    sent(qrecv.at[pl.ds(0, NC - 1)], S_QK)
    sent(mrecv.at[pl.ds(0, NC - 1)], S_MK)
    sent(brecv.at[pl.ds(0, ND // 2 - 1)], S_B)
    sent(brecv.at[pl.ds(0, ND // 2)], S_B2)
    sent(tl_recv.at[pl.ds(0, ND - 1)], S_TL)
    sent(tr_recv.at[pl.ds(0, ND - 1)], S_TR)
    sent(grecv.at[pl.ds(0, NC - 1)], S_G)
    sent(xrecv.at[pl.ds(0, ND - 1)], S_X)


def run(*operands):
    vm = pl.BlockSpec(memory_space=pltpu.VMEM)
    sm = pl.BlockSpec(memory_space=pltpu.SMEM)
    V = pltpu.VMEM
    scratch = [
        V((SQ * CB, 128), F32), V((SQ * CB, 128), F32), V((SQ, CB, 256), BF),
        V((176, 2048), BF), V((2048, 256), BF), V((1024, 128), BF),
        V((528, 128), BF), V((32, 32, 128), BF), V((4, CB, 1024), F32),
        V((SQ, 128), BF), V((SQ, WR), BF), V((2, SQ, WL), BF), V((8, 4, CB, 384), BF),
        V((2048, 1024), BF), V((2816, 256), BF), V((2816, 256), F32),
        V((32, 576, 256), BF), V((576, 1024), F32),
        V((RB, CB, 128), F32), V((RB, 128, 128), BF),
        V((ND * RP, 128), F32), V((8 * RP, 128), F32), V((8, PK, 128), BF),
        V((ND, PK, 128), BF), V((ND, PK, 128), BF),
        V((N, 128), F32), V((4, N, 128), BF), V((4, N, 256), BF), V((CB, N), F32),
        V((NC, 4, CB, 128), BF), V((4, NR * RP, 256), BF), V((4, NR * RP, 256), BF),
        V((NR * RP, 128), F32), V((ND, PK, 128), BF), V((2 * RP, 128), F32),
        V((NR, SQ, WR), BF), V((NR, SQ, WL), BF), V((NC, 4, CB, 384), BF), V((NC, SQ, 128), BF),
        V((ND, PK, 128), BF), V((ND, PK, 128), BF), V((ND, PK, 128), BF), V((NC, 4, CB, 128), BF),
        V((ND, PK, 128), BF),
        pltpu.SemaphoreType.DMA((11,)), pltpu.SemaphoreType.DMA((11,)),
    ]
    return pl.pallas_call(
        kernel,
        out_shape=(
            jax.ShapeDtypeStruct((SQ, CB, 256), BF),
            jax.ShapeDtypeStruct((RB, CB, 128), BF),
        ),
        in_specs=[vm] * 3 + [sm] + [vm] * 12,
        out_specs=(vm, vm),
        scratch_shapes=scratch,
        compiler_params=pltpu.CompilerParams(
            collective_id=0, has_side_effects=True, vmem_limit_bytes=63 << 20
        ),
    )(*operands)


def shards(
    msa, pair, marks, res_marks, ordinals, strand, dist_vectors, w_bias, w_q, w_kv, w_gate, w_mix,
    w_cov, w_opm, w_tri, w_valve, w_exit,
):
    c = lax.axis_index("col")
    code = ordinals + 4096 * strand + 65536 * res_marks
    code_col = jnp.broadcast_to(lax.dynamic_slice_in_dim(code, c * CB, CB)[:, None], (CB, 128))
    return run(
        msa, pair, marks, code, code_col, w_cov.T, w_q, w_kv, w_gate, w_mix, w_opm, dist_vectors,
        w_tri, w_bias.T, w_valve, w_exit,
    )


def solution(mesh):
    placed = (P("row", "col", None), P("row", "col", None), P("row", "col")) + (P(),) * 14
    return jax.shard_map(
        shards,
        mesh=mesh,
        in_specs=placed,
        out_specs=(P("row", "col", None), P("row", "col", None)),
        check_vma=False,
    )
```

time: 219 us -> 162 us (0.74)
  Pallas kernels: 207 us -> 157 us
  local copies, waits for them, and re-layouts: 9.7 us -> 4.52 us
    pallas_call x1, Pallas kernels: 207 us -> 157 us  [run(): pl.pallas_call(kernel, out_shape=(jax.ShapeDtypeStruct((SQ, CB, 256), BF)...]
    unnamed x26 -> x12, local copies, waits for them, and re-layouts: 5.54 us -> 3.75 us
where the time goes in v3:
time: 162 us
  Pallas kernels  157 us (97%)
  local copies, waits for them, and re-layouts  4.52 us (3%)
    pallas_call x1, Pallas kernels, run(): pl.pallas_call(kernel, out_shape=(jax.ShapeDtypeStruct((SQ, CB, 256), BF)...  157 us
    unnamed x12, local copies, waits for them, and re-layouts  3.75 us

profile of v3, /device:TPU:96, one launch (start us, length us, event | category | flops | bytes accessed | tf_op | source)
XLA Modules:
  0.0 162.2 jit_solution(13864227321673881219)
XLA Ops:
  0.6 0.0 copy-start.4
  0.6 0.0 copy-start.3
  0.7 0.0 copy-start.2
  0.7 0.7 copy-done.4
  1.3 0.0 copy-done.3
  1.3 0.0 copy-done.2
  1.4 0.0 copy-start.1
  1.4 0.1 dynamic_slice.3
  1.4 0.7 broadcast_in_dim.2.code_col
  2.1 0.0 copy-done.1
  2.1 157.0 %shard_map.176 = (bf16[16,88,256]{2,1,0:T(8,128)(2,1)}, bf16[44,88,128]{2,1,0:T(8,128)(2,1)}) custom-call(bf16[16,88,256]{2,1,0:T(8,128)(2,1)} %x_ref.1, bf16[44,88,128]{2,1,0:T(8,128)(2,1)} %pair_ref.1, s32[16,88]{1,0:T(8,128)} %marks_ref.1, s32[704]{0:T(1024)} %copy-done.1, s32[88,128]{1,0:T(8,128)} %broadcast_in_dim.2.code_col, bf16[64,256]{1,0:T(8,128)(2,1)} %bitcast.2, ...), custom_call_target="tpu_custom_call" | custom-call | tf_op jit(solution)/shard_map/pallas_call | solution.py:506
  159.1 0.0 copy-start
  159.1 2.1 %copy.21 = bf16[16,88,256]{2,1,0:T(8,128)(2,1)} copy(bf16[16,88,256]{2,1,0:T(8,128)(2,1)} %get-tuple-element.4) | data formatting | bytes 1441792
  161.2 0.0 copy-done
  161.2 0.9 copy.22
  (1 shorter events, 0.0 us)
Async XLA Ops:
  0.6 0.7 copy-start.4
  0.6 0.7 copy-start.3
  0.7 0.7 copy-start.2
  1.4 0.8 copy-start.1
  159.1 2.1 %copy-start = (bf16[44,88,128]{2,1,0:T(8,128)(2,1)S(1)}, bf16[44,88,128]{2,1,0:T(8,128)(2,1)}, u32[]{:S(2)}) copy-start(bf16[44,88,128]{2,1,0:T(8,128)(2,1)} %get-tuple-element.5) | copy-start | bytes 2973700

commit v4 on v3

--- a/solution.py
+++ b/solution.py
@@ -379,19 +379,19 @@
 
     loop(0, NC, attend)
 
-    def unpack_side(recv, buf):
+    def unpack_side(recv, buf, low, high):
         def step(q):
             for b in range(NC):
                 tile = jnp.concatenate(unpack(recv[q * NC + b].astype(F32)), axis=0).astype(BF)
                 buf[b // 2, pl.ds(pl.multiple_of(RP * q, 16), RP), 128 * (b % 2) : 128 * (b % 2) + 128] = tile
 
-        loop(0, NR, step)
+        loop(low, high, step)
 
     arrived(tl_recv, S_TL)
-    unpack_side(tl_recv, lbuf)
+    unpack_side(tl_recv, lbuf, 0, NR)
     arrived(tr_recv, S_TR)
-    unpack_side(tr_recv, rbuf)
     for pair in range(4):
+        unpack_side(tr_recv, rbuf, 4 * pair, 4 * pair + 4)
         total = None
         for b in range(4):
             y = dot_nt(lbuf[b], rbuf[b, 4 * RP * pair : 4 * RP * pair + 4 * RP, :])
@@ -421,6 +421,17 @@
             def _():
                 send(tout.at[rr * NC + cc], xrecv.at[me], S_X, rr, cc)
 
+    def pair_gate(first, lanes):
+        def step(k):
+            xs[pl.ds(pl.multiple_of(CB * k, 8), CB), lanes : lanes + 128] = jax.nn.sigmoid(
+                dot(hb[first + k], w_valve[...])[:CB]
+            )
+
+        return step
+
+    loop(0, 32, pair_gate(0, 0), 4)
+    loop(0, RB - 32, pair_gate(32, 128), 4)
+
     arrived(grecv, S_G)
     w_rep = []
     for h in range(8):
@@ -431,7 +442,7 @@
         cat = jnp.concatenate([grecv[h, sg].astype(F32) for h in range(8)], axis=1) * gates[sg]
         for t in range(4):
             y = dot(jnp.where(wide_group == t, cat, 0.0).astype(BF), w_rep)
-            out_a[4 * sg + t] = (x_ref[4 * sg + t].astype(F32) + y).astype(BF)
+            out_a[4 * sg + t] = y
 
     loop(0, 4, mix)
 
@@ -452,13 +463,18 @@
     stats[0:RP, :] = mean
     stats[RP:, :] = lax.rsqrt(total * (1.0 / 128) + norm_eps)
 
-    def last(i):
-        cross = (st[pl.ds(i, 128, stride=RP), :] - stats[pl.ds(i, 1), :]) * stats[pl.ds(RP + i, 1), :]
-        proj = dot_tn(cross.astype(BF), w_exit[...])[:CB]
-        gate = jax.nn.sigmoid(dot(hb[i], w_valve[...])[:CB])
-        out_b[i] = (zscr[i] + gate * proj).astype(BF)
-
-    loop(0, RB, last, 2)
+    def last(first, lanes):
+        def step(k):
+            i = first + k
+            cross = (st[pl.ds(i, 128, stride=RP), :] - stats[pl.ds(i, 1), :]) * stats[pl.ds(RP + i, 1), :]
+            proj = dot_tn(cross.astype(BF), w_exit[...])[:CB]
+            gate = xs[pl.ds(pl.multiple_of(CB * k, 8), CB), lanes : lanes + 128]
+            out_b[i] = (zscr[i] + gate * proj).astype(BF)
+
+        return step
+
+    loop(0, 32, last(0, 0), 4)
+    loop(0, RB - 32, last(32, 128), 4)
 
     sent(rall.at[pl.ds(0, 7)], S_R)
     sent(rall.at[pl.ds(0, 8)], S_R2)
@@ -506,7 +522,7 @@
     return pl.pallas_call(
         kernel,
         out_shape=(
-            jax.ShapeDtypeStruct((SQ, CB, 256), BF),
+            jax.ShapeDtypeStruct((SQ, CB, 256), F32),
             jax.ShapeDtypeStruct((RB, CB, 128), BF),
         ),
         in_specs=[vm] * 3 + [sm] + [vm] * 12,
@@ -525,10 +541,11 @@
     c = lax.axis_index("col")
     code = ordinals + 4096 * strand + 65536 * res_marks
     code_col = jnp.broadcast_to(lax.dynamic_slice_in_dim(code, c * CB, CB)[:, None], (CB, 128))
-    return run(
+    change, pair_out = run(
         msa, pair, marks, code, code_col, w_cov.T, w_q, w_kv, w_gate, w_mix, w_opm, dist_vectors,
         w_tri, w_bias.T, w_valve, w_exit,
     )
+    return (msa.astype(F32) + change).astype(BF), pair_out
 
 
 def solution(mesh):

time: 162 us -> 161 us (level)
  other arithmetic: 0.01 us -> 3.19 us
  local copies, waits for them, and re-layouts: 4.52 us -> 1.73 us
  Pallas kernels: 157 us -> 155 us
    unnamed x12 -> x7, local copies, waits for them, and re-layouts: 3.75 us -> 0.96 us
    convert_element_type x0 -> x1, other arithmetic: none -> 2.46 us  [shards(): return ((msa.astype(F32) + change).astype(BF), pair_out)]
    pallas_call x1, Pallas kernels: 157 us -> 155 us  [run(): pl.pallas_call(kernel, out_shape=(jax.ShapeDtypeStruct((SQ, CB, 256), F32...]
where the time goes in v4:
time: 161 us; the launch traced here: 160 us
  Pallas kernels  155 us (96%)
  other arithmetic  3.19 us (2%)
  local copies, waits for them, and re-layouts  1.73 us (1%)
    pallas_call x1, Pallas kernels, run(): pl.pallas_call(kernel, out_shape=(jax.ShapeDtypeStruct((SQ, CB, 256), F32...  155 us

profile of v4, /device:TPU:96, one launch (start us, length us, event | category | flops | bytes accessed | tf_op | source)
XLA Modules:
  0.0 160.4 jit_solution(3633321456334965627)
XLA Ops:
  0.6 0.7 multiply_add_fusion.code_ref
  1.4 0.0 copy-start.2
  1.4 0.1 dynamic_slice.3
  1.4 0.7 broadcast_in_dim.2.code_col
  2.1 0.0 copy-done.2
  2.1 0.0 copy-start
  2.1 154.8 %shard_map.176 = (f32[16,88,256]{2,1,0:T(8,128)}, bf16[44,88,128]{2,1,0:T(8,128)(2,1)}) custom-call(bf16[16,88,256]{2,1,0:T(8,128)(2,1)} %x_ref.1, bf16[44,88,128]{2,1,0:T(8,128)(2,1)} %pair_ref.1, s32[16,88]{1,0:T(8,128)} %marks_ref.1, s32[704]{0:T(1024)} %copy-done.2, s32[88,128]{1,0:T(8,128)} %broadcast_in_dim.2.code_col, bf16[64,256]{1,0:T(8,128)(2,1)} %bitcast.2, ...), custom_call_target="tpu_custom_call" | custom-call | tf_op jit(solution)/shard_map/pallas_call | solution.py:522
  156.9 0.0 copy-done
  156.9 0.0 copy-start.1
  157.0 2.5 %add_convert_fusion = bf16[16,88,256]{2,1,0:T(8,128)(2,1)} fusion(f32[16,88,256]{2,1,0:T(8,128)} %get-tuple-element.4, bf16[16,88,256]{2,1,0:T(8,128)(2,1)S(1)} %copy-done), kind=kLoop, calls=%fused_computation | loop fusion | flops 1081344 | bytes 2883584 | tf_op jit(solution)/shard_map/convert_element_type | solution.py:548
  159.4 0.0 copy-done.1
  159.4 0.9 copy.20
Async XLA Ops:
  1.4 0.8 copy-start.2
  2.1 154.8 %copy-start = (bf16[16,88,256]{2,1,0:T(8,128)(2,1)S(1)}, bf16[16,88,256]{2,1,0:T(8,128)(2,1)}, u32[]{:S(2)}) copy-start(bf16[16,88,256]{2,1,0:T(8,128)(2,1)} %x_ref.1) | copy-start | bytes 2162692
  156.9 2.5 %copy-start.1 = (bf16[44,88,128]{2,1,0:T(8,128)(2,1)S(1)}, bf16[44,88,128]{2,1,0:T(8,128)(2,1)}, u32[]{:S(2)}) copy-start(bf16[44,88,128]{2,1,0:T(8,128)(2,1)} %get-tuple-element.9) | copy-start | bytes 2973700
